TPU v7x, 512 devices: a whole 4x4x16 slice. The times are simulated.
512 devices in a mesh: section: 8 (over x, core), expert: 64 (over y, z).
Axes of the slice: x: 4, y: 4, z: 16, core: 2. Of those that a mesh axis runs over, the one named last changes fastest.
Arguments:
- entering: bfloat16 [8, 2048, 3584], P('section', 'expert'), may hold values from -6 to 6
- saved: bfloat16 [8, 64, 384, 384], P('section', 'expert'), may hold values from -6 to 6
- routes: int32 [2, 8, 2048, 1], P(None, 'section', 'expert'), may hold values from 0 to 7; in each aligned block of 32 rows (0 to 31, 32 to 63, ..., all dimensions but the last counted through in order) at most 6 rows name the same one
- gates: float32 [2, 8, 2048, 1], P(None, 'section', 'expert'), may hold values from 0.1 to 1
- w_in: bfloat16 [8, 64, 3584, 384], P('section', 'expert'), may hold values from -0.09375 to 0.09375
- w_out: bfloat16 [8, 64, 192, 3584], P('section', 'expert'), may hold values from -0.15625 to 0.15625
Outputs:
- results: bfloat16 [2, 8, 2048, 3584], P(None, 'section', 'expert')
Inputs may be any that keep to these rules, and one draw needn't show every extreme that they name: `routes`: each row names one expert; in the rows of one device for one tick and layer no expert is named more than 6 times.
All inputs are finite; a program needn't handle non-finite values.
Results may differ from a plain program's by a relative error of at most 0.015.
Values may be sent and summed in bfloat16 or wider, within the bound.
No kernel may reach another device: no remote copies, remote signals or barrier semaphores. Data moves between devices by JAX's collectives and lax.ppermute only.
A program may use at most 64 MiB of HBM per device.

v0:
```python
import jax
import jax.numpy as jnp
from jax import lax
from jax.sharding import PartitionSpec as P

SHARDS = 8


def shifted(shard, axis, by):
    devices = lax.axis_size(axis)
    pairs = [(i, i + by) for i in range(devices) if 0 <= i + by < devices]
    return lax.ppermute(shard, axis, pairs)


def silu_slope(gate_vals):
    sigmoid_vals = jax.nn.sigmoid(gate_vals)
    return sigmoid_vals * (1.0 + gate_vals * (1.0 - sigmoid_vals))


def routing_tables(routes, weights, experts, capacity):
    tok_count, top_count = routes.shape
    pair_count = tok_count * top_count
    flat_routes = routes.reshape(pair_count)
    expert_ids = jnp.arange(experts, dtype=jnp.int32)
    onehot = (flat_routes[:, None] == expert_ids[None, :]).astype(jnp.float32)
    pair_ids = jnp.arange(pair_count, dtype=jnp.int32)
    earlier = (pair_ids[None, :] < pair_ids[:, None]).astype(jnp.float32)
    before = jnp.dot(earlier, onehot, precision=lax.Precision.HIGHEST)
    slot_ids = jnp.sum(before * onehot, axis=1).astype(jnp.int32)
    targets = flat_routes * capacity + slot_ids
    slot_range = jnp.arange(experts * capacity, dtype=jnp.int32)
    places = (slot_range[:, None] == targets[None, :]).astype(jnp.float32)
    token_ids = jnp.arange(tok_count, dtype=jnp.int32)
    owners = ((pair_ids // top_count)[:, None] == token_ids[None, :]).astype(jnp.float32)
    sending = jnp.dot(places, owners, precision=lax.Precision.HIGHEST).astype(jnp.bfloat16)
    weighted = owners * weights.reshape(pair_count)[:, None]
    mixing = lax.dot_general(
        weighted, places, (((0,), (1,)), ((), ())), precision=lax.Precision.HIGHEST
    )
    return (sending, mixing)


def expert_forward(token_rows, w_in_dev, w_out_dev):
    pre_act = jnp.dot(token_rows, w_in_dev, preferred_element_type=jnp.float32)
    half_width = w_out_dev.shape[0]
    gate_vals = pre_act[:, :half_width]
    up_vals = pre_act[:, half_width:]
    hidden = (jax.nn.silu(gate_vals) * up_vals).astype(jnp.bfloat16)
    return jnp.dot(hidden, w_out_dev, preferred_element_type=jnp.float32).astype(jnp.bfloat16)


def expert_backward(grad_rows, saved_pre, w_in_dev, w_out_dev):
    half_width = w_out_dev.shape[0]
    gate_vals = saved_pre[:, :half_width].astype(jnp.float32)
    up_vals = saved_pre[:, half_width:].astype(jnp.float32)
    d_hidden = lax.dot_general(
        grad_rows, w_out_dev, (((1,), (1,)), ((), ())), preferred_element_type=jnp.float32
    )
    d_gate = d_hidden * up_vals * silu_slope(gate_vals)
    d_up = d_hidden * jax.nn.silu(gate_vals)
    d_pre = jnp.concatenate([d_gate, d_up], axis=1).astype(jnp.bfloat16)
    return lax.dot_general(
        d_pre, w_in_dev, (((1,), (1,)), ((), ())), preferred_element_type=jnp.float32
    ).astype(jnp.bfloat16)


def shards(entering, saved, routes, gates, w_in, w_out):
    peer_count = lax.axis_size("expert")
    experts = peer_count // SHARDS
    tok_count = entering.shape[1]
    row_width = entering.shape[2]
    top_count = routes.shape[3]
    capacity = min(
        tok_count, max(2, (3 * tok_count * top_count + 2 * experts - 1) // (2 * experts))
    )
    w_in_dev = w_in[0, 0]
    w_out_dev = w_out[0, 0]
    saved_dev = saved[0, 0]
    section_idx = lax.axis_index("section")
    forward_first = section_idx % 2 == 0
    current = entering[0]
    collected = []

    def run_forward(arrived_rows):
        return expert_forward(arrived_rows, w_in_dev, w_out_dev)

    def run_backward(arrived_rows):
        return expert_backward(arrived_rows, saved_dev, w_in_dev, w_out_dev)

    for tick_idx in range(2):
        doing_forward = forward_first if tick_idx == 0 else jnp.logical_not(forward_first)
        sending, mixing = routing_tables(routes[tick_idx, 0], gates[tick_idx, 0], experts, capacity)
        token_rows = jnp.dot(sending, current, preferred_element_type=jnp.float32).astype(
            jnp.bfloat16
        )
        shaped = token_rows.reshape(experts, 1, capacity, row_width)
        copies = jnp.broadcast_to(shaped, (experts, SHARDS, capacity, row_width)).reshape(
            peer_count, capacity, row_width
        )
        arrived = lax.all_to_all(copies, "expert", split_axis=0, concat_axis=0, tiled=True)
        expert_out = lax.cond(
            doing_forward,
            run_forward,
            run_backward,
            arrived.reshape(peer_count * capacity, row_width),
        )
        returned = lax.all_to_all(
            expert_out.reshape(peer_count, capacity, row_width),
            "expert",
            split_axis=0,
            concat_axis=0,
            tiled=True,
        )
        summed = jnp.sum(
            returned.reshape(experts, SHARDS, capacity, row_width).astype(jnp.float32), axis=1
        )
        mixed_sum = jnp.dot(
            mixing, summed.reshape(experts * capacity, row_width), precision=lax.Precision.HIGHEST
        )
        layer_result = (current.astype(jnp.float32) + mixed_sum).astype(jnp.bfloat16)
        collected.append(layer_result)
        if tick_idx == 0:
            from_below = shifted(layer_result, "section", 1)
            from_above = shifted(layer_result, "section", -1)
            current = jnp.where(forward_first, from_above, from_below)
    return jnp.stack(collected)[:, None]


def solution(mesh):
    return jax.shard_map(
        shards,
        mesh=mesh,
        in_specs=(
            P("section", "expert", None),
            P("section", "expert", None, None),
            P(None, "section", "expert", None),
            P(None, "section", "expert", None),
            P("section", "expert", None, None),
            P("section", "expert", None, None),
        ),
        out_specs=P(None, "section", "expert", None),
        check_vma=False,
    )
```

profile of v0, /device:TPU:2, one launch (start us, length us, event | category | flops | bytes accessed | tf_op | source)
XLA Modules:
  0.0 762.6 jit_solution(14235250974928074675)
XLA Ops:
  0.0 0.7 slice_bitcast_fusion.2
  0.7 0.1 fusion.39
  0.8 0.1 fusion.40
  1.0 0.7 convert_add_fusion.1
  1.6 0.1 convolution_convert_fusion.3
  1.8 1.2 convolution_convert_fusion.1
  2.9 0.1 broadcast_in_dim.10
  3.1 2.1 broadcast_in_dim.11
  5.2 19.1 %all-to-all-start = ((bf16[64,6,3584]{2,1,0:T(8,128)(2,1)}), bf16[64,6,3584]{2,1,0:T(8,128)(2,1)}, u32[]{:S(2)}, u32[]{:S(2)}) async-start(bf16[64,6,3584]{2,1,0:T(8,128)(2,1)} %bitcast.52), calls=%async_computation | async-start | bytes 7340032 | tf_op jit(solution)/shard_map/all_to_all | solution.py:100
  24.3 0.2 copy.9
  24.5 0.0 copy-start.3
  24.5 0.0 copy-start
  24.5 165.4 %all-to-all-done = bf16[64,6,3584]{2,1,0:T(8,128)(2,1)} async-done(((bf16[64,6,3584]{2,1,0:T(8,128)(2,1)}), bf16[64,6,3584]{2,1,0:T(8,128)(2,1)}, u32[]{:S(2)}, u32[]{:S(2)}) %all-to-all-start) | async-done | bytes 2752544 | tf_op jit(solution)/shard_map/all_to_all | solution.py:100
  190.0 5.5 reshape.58
  195.5 6.7 conditional.4
  195.5 4.2 fusion.59
  199.7 2.5 fusion.15
  202.2 5.4 reshape.59
  207.6 7.5 all-to-all-start.1
  215.2 0.3 fusion.44
  215.4 0.0 copy-start.1
  215.5 164.4 %all-to-all-done.1 = bf16[64,6,3584]{2,1,0:T(8,128)(2,1)} async-done(((bf16[64,6,3584]{2,1,0:T(8,128)(2,1)}), bf16[64,6,3584]{2,1,0:T(8,128)(2,1)}, u32[]{:S(2)}, u32[]{:S(2)}) %all-to-all-start.1) | async-done | bytes 2752544 | tf_op jit(solution)/shard_map/all_to_all | solution.py:107
  379.9 2.9 convert_reduce_fusion.1
  382.7 0.1 reshape.60
  382.9 0.5 fusion.38
  383.4 1.9 collective-permute-start
  385.3 2.4 collective-permute-start.1
  387.7 0.1 convolution_convert_fusion.2
  387.9 1.0 collective-permute-done
  388.8 3.8 collective-permute-done.1
  392.7 0.2 convolution_convert_fusion
  392.9 0.1 broadcast_in_dim.12
  393.0 2.1 broadcast_in_dim.13
  395.1 7.7 %all-to-all-start.2 = ((bf16[64,6,3584]{2,1,0:T(8,128)(2,1)}), bf16[64,6,3584]{2,1,0:T(8,128)(2,1)}, u32[]{:S(2)}, u32[]{:S(2)}) async-start(bf16[64,6,3584]{2,1,0:T(8,128)(2,1)} %bitcast.53), calls=%async_computation.2 | async-start | bytes 7340032 | tf_op jit(solution)/shard_map/all_to_all | solution.py:100
  402.8 0.0 copy-start.4
  402.8 164.7 %all-to-all-done.2 = bf16[64,6,3584]{2,1,0:T(8,128)(2,1)} async-done(((bf16[64,6,3584]{2,1,0:T(8,128)(2,1)}), bf16[64,6,3584]{2,1,0:T(8,128)(2,1)}, u32[]{:S(2)}, u32[]{:S(2)}) %all-to-all-start.2) | async-done | bytes 2752544 | tf_op jit(solution)/shard_map/all_to_all | solution.py:100
  567.6 5.5 reshape.62
  573.0 6.2 conditional.5
  573.0 3.0 fusion.25
  576.1 3.2 fusion.28
  579.3 5.4 reshape.63
  584.7 7.7 %all-to-all-start.3 = ((bf16[64,6,3584]{2,1,0:T(8,128)(2,1)}), bf16[64,6,3584]{2,1,0:T(8,128)(2,1)}, u32[]{:S(2)}, u32[]{:S(2)}) async-start(bf16[64,6,3584]{2,1,0:T(8,128)(2,1)} %reshape.63), calls=%async_computation.3 | async-start | bytes 7340032 | tf_op jit(solution)/shard_map/all_to_all | solution.py:107
  592.3 0.3 fusion.43
  592.6 165.7 %all-to-all-done.3 = bf16[64,6,3584]{2,1,0:T(8,128)(2,1)} async-done(((bf16[64,6,3584]{2,1,0:T(8,128)(2,1)}), bf16[64,6,3584]{2,1,0:T(8,128)(2,1)}, u32[]{:S(2)}, u32[]{:S(2)}) %all-to-all-start.3) | async-done | bytes 2752544 | tf_op jit(solution)/shard_map/all_to_all | solution.py:107
  758.3 2.9 convert_reduce_fusion
  761.1 0.1 reshape.64
  761.3 0.5 fusion.41
  761.8 0.8 maximum_bitcast_fusion
  (11 shorter events, 0.0 us)
Async XLA Ops:
  5.2 19.1 %copy-start.2 = (bf16[1,1,384,384]{3,2,1,0:T(8,128)(2,1)S(1)}, bf16[1,1,384,384]{3,2,1,0:T(8,128)(2,1)}, u32[]{:S(2)}) copy-start(bf16[1,1,384,384]{3,2,1,0:T(8,128)(2,1)} %param.11) | copy-start | bytes 884740
  5.2 184.8 %all-to-all-start = ((bf16[64,6,3584]{2,1,0:T(8,128)(2,1)}), bf16[64,6,3584]{2,1,0:T(8,128)(2,1)}, u32[]{:S(2)}, u32[]{:S(2)}) async-start(bf16[64,6,3584]{2,1,0:T(8,128)(2,1)} %bitcast.52), calls=%async_computation | async-start | bytes 7340032 | tf_op jit(solution)/shard_map/all_to_all | solution.py:100
  24.5 170.9 %copy-start.3 = (bf16[1,1,384,384]{2,3,1,0:T(8,128)(2,1)}, bf16[1,1,384,384]{2,3,1,0:T(8,128)(2,1)S(1)}, u32[]{:S(2)}) copy-start(bf16[1,1,384,384]{2,3,1,0:T(8,128)(2,1)S(1)} %copy.9) | copy-start | bytes 884740
  24.5 170.9 %copy-start = (bf16[1,1,192,3584]{3,2,1,0:T(8,128)(2,1)S(1)}, bf16[1,1,192,3584]{3,2,1,0:T(8,128)(2,1)}, u32[]{:S(2)}) copy-start(bf16[1,1,192,3584]{3,2,1,0:T(8,128)(2,1)} %param.15) | copy-start | bytes 4128772
  207.6 7.6 copy-start.5
  207.6 172.3 %all-to-all-start.1 = ((bf16[64,6,3584]{2,1,0:T(8,128)(2,1)}), bf16[64,6,3584]{2,1,0:T(8,128)(2,1)}, u32[]{:S(2)}, u32[]{:S(2)}) async-start(bf16[64,6,3584]{2,1,0:T(8,128)(2,1)} %reshape.59), calls=%async_computation.1 | async-start | bytes 7340032 | tf_op jit(solution)/shard_map/all_to_all | solution.py:107
  215.4 167.4 %copy-start.1 = (bf16[1,32,3584]{2,1,0:T(8,128)(2,1)S(1)}, bf16[1,32,3584]{2,1,0:T(8,128)(2,1)}, u32[]{:S(2)}) copy-start(bf16[1,32,3584]{2,1,0:T(8,128)(2,1)} %param.10) | copy-start | bytes 688132
  383.4 5.4 collective-permute-start
  385.3 7.3 collective-permute-start.1
  395.1 172.4 %all-to-all-start.2 = ((bf16[64,6,3584]{2,1,0:T(8,128)(2,1)}), bf16[64,6,3584]{2,1,0:T(8,128)(2,1)}, u32[]{:S(2)}, u32[]{:S(2)}) async-start(bf16[64,6,3584]{2,1,0:T(8,128)(2,1)} %bitcast.53), calls=%async_computation.2 | async-start | bytes 7340032 | tf_op jit(solution)/shard_map/all_to_all | solution.py:100
  402.8 170.2 %copy-start.4 = (bf16[1,1,384,384]{2,3,1,0:T(8,128)(2,1)S(1)}, bf16[1,1,384,384]{2,3,1,0:T(8,128)(2,1)}, u32[]{:S(2)}) copy-start(bf16[1,1,384,384]{2,3,1,0:T(8,128)(2,1)} %copy-done.3) | copy-start | bytes 884740
  573.0 3.0 copy-start.7
  584.7 173.6 %all-to-all-start.3 = ((bf16[64,6,3584]{2,1,0:T(8,128)(2,1)}), bf16[64,6,3584]{2,1,0:T(8,128)(2,1)}, u32[]{:S(2)}, u32[]{:S(2)}) async-start(bf16[64,6,3584]{2,1,0:T(8,128)(2,1)} %reshape.63), calls=%async_computation.3 | async-start | bytes 7340032 | tf_op jit(solution)/shard_map/all_to_all | solution.py:107
where the time goes:
time: 764 us; the launch traced here: 763 us
  waiting for transfers between devices  665 us (87%)
  starting transfers between devices  46.3 us (6%)
  local copies, waits for them, and re-layouts  27.3 us (4%)
  matrix products  16.5 us (2%)
    all_to_all x2, waiting for transfers between devices, shards(): lax.all_to_all(copies, 'expert', split_axis=0, concat_axis=0, tiled=True)  330 us
    all_to_all x2, waiting for transfers between devices, shards(): lax.all_to_all(expert_out.reshape(peer_count, capacity, row_width), 'expe...  330 us
    all_to_all x2, starting transfers between devices, shards(): lax.all_to_all(copies, 'expert', split_axis=0, concat_axis=0, tiled=True)  26.8 us
  transfers between devices with their start and end apart: 6, of which 6 were waited for; matrix products, arithmetic and copies ran while one was open for 0% of the time, Pallas kernels for 0%

commit v1 on v0

--- a/solution.py
+++ b/solution.py
@@ -17,27 +17,16 @@
     return sigmoid_vals * (1.0 + gate_vals * (1.0 - sigmoid_vals))
 
 
-def routing_tables(routes, weights, experts, capacity):
-    tok_count, top_count = routes.shape
-    pair_count = tok_count * top_count
-    flat_routes = routes.reshape(pair_count)
-    expert_ids = jnp.arange(experts, dtype=jnp.int32)
-    onehot = (flat_routes[:, None] == expert_ids[None, :]).astype(jnp.float32)
-    pair_ids = jnp.arange(pair_count, dtype=jnp.int32)
-    earlier = (pair_ids[None, :] < pair_ids[:, None]).astype(jnp.float32)
-    before = jnp.dot(earlier, onehot, precision=lax.Precision.HIGHEST)
-    slot_ids = jnp.sum(before * onehot, axis=1).astype(jnp.int32)
+def routing_places(routes, experts, capacity):
+    tok_count = routes.shape[0]
+    flat_routes = routes.reshape(tok_count)
+    token_ids = jnp.arange(tok_count, dtype=jnp.int32)
+    same = flat_routes[:, None] == flat_routes[None, :]
+    earlier = token_ids[None, :] < token_ids[:, None]
+    slot_ids = jnp.sum(jnp.where(same & earlier, 1, 0), axis=1).astype(jnp.int32)
     targets = flat_routes * capacity + slot_ids
     slot_range = jnp.arange(experts * capacity, dtype=jnp.int32)
-    places = (slot_range[:, None] == targets[None, :]).astype(jnp.float32)
-    token_ids = jnp.arange(tok_count, dtype=jnp.int32)
-    owners = ((pair_ids // top_count)[:, None] == token_ids[None, :]).astype(jnp.float32)
-    sending = jnp.dot(places, owners, precision=lax.Precision.HIGHEST).astype(jnp.bfloat16)
-    weighted = owners * weights.reshape(pair_count)[:, None]
-    mixing = lax.dot_general(
-        weighted, places, (((0,), (1,)), ((), ())), precision=lax.Precision.HIGHEST
-    )
-    return (sending, mixing)
+    return (slot_range[:, None] == targets[None, :]).astype(jnp.bfloat16)
 
 
 def expert_forward(token_rows, w_in_dev, w_out_dev):
@@ -75,7 +64,11 @@
     )
     w_in_dev = w_in[0, 0]
     w_out_dev = w_out[0, 0]
-    saved_dev = saved[0, 0]
+    ring = list(range(0, SHARDS, 2)) + list(range(SHARDS - 1, 0, -2))
+    slice_groups = [[e * SHARDS + j for j in ring] for e in range(experts)]
+    expert_groups = [[e * SHARDS + j for e in range(experts)] for j in range(SHARDS)]
+    saved_dev = saved[0, 0].reshape(experts, SHARDS, capacity, -1)
+    saved_dev = jnp.stack([saved_dev[:, j] for j in ring]).reshape(peer_count * capacity, -1)
     section_idx = lax.axis_index("section")
     forward_first = section_idx % 2 == 0
     current = entering[0]
@@ -87,37 +80,42 @@
     def run_backward(arrived_rows):
         return expert_backward(arrived_rows, saved_dev, w_in_dev, w_out_dev)
 
+    places = [routing_places(routes[t, 0], experts, capacity) for t in range(2)]
     for tick_idx in range(2):
         doing_forward = forward_first if tick_idx == 0 else jnp.logical_not(forward_first)
-        sending, mixing = routing_tables(routes[tick_idx, 0], gates[tick_idx, 0], experts, capacity)
-        token_rows = jnp.dot(sending, current, preferred_element_type=jnp.float32).astype(
+        placed = places[tick_idx]
+        token_rows = jnp.dot(placed, current, preferred_element_type=jnp.float32).astype(
             jnp.bfloat16
         )
-        shaped = token_rows.reshape(experts, 1, capacity, row_width)
-        copies = jnp.broadcast_to(shaped, (experts, SHARDS, capacity, row_width)).reshape(
-            peer_count, capacity, row_width
-        )
-        arrived = lax.all_to_all(copies, "expert", split_axis=0, concat_axis=0, tiled=True)
-        expert_out = lax.cond(
-            doing_forward,
-            run_forward,
-            run_backward,
-            arrived.reshape(peer_count * capacity, row_width),
-        )
-        returned = lax.all_to_all(
-            expert_out.reshape(peer_count, capacity, row_width),
+        exchanged = lax.all_to_all(
+            token_rows.reshape(experts, capacity, row_width),
             "expert",
             split_axis=0,
             concat_axis=0,
+            axis_index_groups=expert_groups,
             tiled=True,
+        ).reshape(experts * capacity, row_width)
+        arrived = lax.all_gather(
+            exchanged, "expert", axis=0, axis_index_groups=slice_groups, tiled=True
         )
-        summed = jnp.sum(
-            returned.reshape(experts, SHARDS, capacity, row_width).astype(jnp.float32), axis=1
+        expert_out = lax.cond(doing_forward, run_forward, run_backward, arrived)
+        summed = lax.psum_scatter(
+            expert_out, "expert", scatter_dimension=0, axis_index_groups=slice_groups, tiled=True
         )
-        mixed_sum = jnp.dot(
-            mixing, summed.reshape(experts * capacity, row_width), precision=lax.Precision.HIGHEST
+        returned = lax.all_to_all(
+            summed.reshape(experts, capacity, row_width),
+            "expert",
+            split_axis=0,
+            concat_axis=0,
+            axis_index_groups=expert_groups,
+            tiled=True,
+        ).reshape(experts * capacity, row_width)
+        picked = lax.dot_general(
+            placed, returned, (((0,), (0,)), ((), ())), preferred_element_type=jnp.float32
         )
-        layer_result = (current.astype(jnp.float32) + mixed_sum).astype(jnp.bfloat16)
+        layer_result = (
+            current.astype(jnp.float32) + gates[tick_idx, 0, :, :] * picked
+        ).astype(jnp.bfloat16)
         collected.append(layer_result)
         if tick_idx == 0:
             from_below = shifted(layer_result, "section", 1)

time: 764 us -> 482 us (0.63)
  the two profiles are of different devices: /device:TPU:2 before, /device:TPU:32 now
where the time goes in v1:
time: 482 us
  waiting for transfers between devices  310 us (64%)
  blocking collectives  119 us (25%)
  starting transfers between devices  16.1 us (3%)
  matrix products  15 us (3%)
  between operations  13.3 us (3%)
  local copies, waits for them, and re-layouts  6.4 us (1%)
    reduce_scatter x2, waiting for transfers between devices, shards(): lax.psum_scatter(expert_out, 'expert', scatter_dimension=0, axis_index_gr...  143 us
    all_gather x2, waiting for transfers between devices, shards(): lax.all_gather(exchanged, 'expert', axis=0, axis_index_groups=slice_group...  131 us
    all_to_all x2, blocking collectives, shards(): lax.all_to_all(token_rows.reshape(experts, capacity, row_width), 'expert'...  73.8 us
    all_to_all x1, blocking collectives, shards(): lax.all_to_all(summed.reshape(experts, capacity, row_width), 'expert', sp...  45.4 us
    all_to_all x1, waiting for transfers between devices, shards(): lax.all_to_all(summed.reshape(experts, capacity, row_width), 'expert', sp...  32.7 us
    all_to_all x1, starting transfers between devices, shards(): lax.all_to_all(summed.reshape(experts, capacity, row_width), 'expert', sp...  12.9 us
  transfers between devices with their start and end apart: 7, of which 6 were waited for; matrix products, arithmetic and copies ran while one was open for 0% of the time, Pallas kernels for 0%

profile of v1, /device:TPU:32, one launch (start us, length us, event | category | flops | bytes accessed | tf_op | source)
XLA Modules:
  0.0 481.7 jit_solution(2508809712628993907)
XLA Ops:
  6.5 0.0 all-gather.3.cloned.1.call-start
  6.5 0.7 slice_bitcast_fusion.8
  7.3 0.2 select_reduce_fusion
  7.4 0.7 multiply_add_fusion
  8.1 1.3 convolution_convert_fusion.1
  9.4 0.1 reshape.49
  9.5 49.5 %all_to_all.20 = bf16[8,6,3584]{2,1,0:T(8,128)(2,1)S(1)} all-to-all(bf16[8,6,3584]{2,1,0:T(8,128)(2,1)S(1)} %reshape.49), channel_id=1, replica_groups={{0,8,16,24,32,40,48,56},{1,9,17,25,33,41,49,57},{2,10,18,26,34,42,50,58..., dimensions={0} | all-to-all | bytes 688128 | tf_op jit(solution)/shard_map/all_to_all | solution.py:90
  59.0 0.8 reshape.50
  59.9 0.0 all-gather.3.cloned.1.call-update
  59.9 0.0 reduce-scatter.3.cloned.1.call-start
  60.0 0.1 reshape_squeeze.10
  60.2 0.1 reshape.51
  60.3 63.3 %all-gather.3.cloned.1.call-done = bf16[384,3584]{1,0:T(8,128)(2,1)} async-done(((bf16[48,3584]{1,0:T(8,128)(2,1)}), bf16[384,3584]{1,0:T(8,128)(2,1)}) %all-gather.3.cloned.1.call-update) | async-done | bytes 2752528 | tf_op jit(solution)/shard_map/all_gather | solution.py:98
  123.6 6.8 %conditional.4 = (bf16[384,3584]{1,0:T(8,128)(2,1)}) conditional(s32[]{:T(128)} %convert_element_type.57, (bf16[384,3584]{1,0:T(8,128)(2,1)}, bf16[192,3584]{1,0:T(8,128)(2,1)S(1)}, bf16[384,384]{1,0:T(8,128)(2,1)S(1)}, bf16[3584,384]{1,0:T(8,128)(2,1)}) %tuple.53, (bf16[384,3584]{1,0:T(8,128)(2,1)}, bf16[3584,384]{1,0:T(8,128)(2,1)}, ...), branch_computations={%region_1.2_spmd, %region_2.3_spmd} | conditional | flops 1587142656 | bytes 22118436
  123.6 4.2 fusion.56
  127.9 2.5 fusion.15
  130.4 0.0 reduce-scatter.3.cloned.1.call-update
  130.4 71.5 %reduce-scatter.3.cloned.1.call-done = bf16[48,3584]{1,0:T(8,128)(2,1)} async-done(((bf16[384,3584]{1,0:T(8,128)(2,1)}), bf16[48,3584]{1,0:T(8,128)(2,1)}) %reduce-scatter.3.cloned.1.call-update) | async-done | bytes 344080 | tf_op jit(solution)/shard_map/reduce_scatter | solution.py:102
  201.9 1.9 reshape.52
  203.7 12.9 %all-to-all-start.1 = ((bf16[8,6,3584]{2,1,0:T(8,128)(2,1)}), bf16[8,6,3584]{2,1,0:T(8,128)(2,1)S(1)}, u32[]{:S(2)}, u32[]{:S(2)}) async-start(bf16[8,6,3584]{2,1,0:T(8,128)(2,1)} %reshape.52), calls=%async_computation.2 | async-start | bytes 917504 | tf_op jit(solution)/shard_map/all_to_all | solution.py:105
  216.6 0.0 all-gather.5.cloned.1.call-start
  216.7 0.0 copy-done.3
  216.7 32.7 %all-to-all-done.1 = bf16[8,6,3584]{2,1,0:T(8,128)(2,1)S(1)} async-done(((bf16[8,6,3584]{2,1,0:T(8,128)(2,1)}), bf16[8,6,3584]{2,1,0:T(8,128)(2,1)S(1)}, u32[]{:S(2)}, u32[]{:S(2)}) %all-to-all-start.1) | async-done | bytes 344096 | tf_op jit(solution)/shard_map/all_to_all | solution.py:105
  249.4 0.1 reshape.53
  249.6 0.3 fusion.39
  249.8 1.8 collective-permute-start.1
  251.6 1.3 collective-permute-start
  252.9 0.0 collective-permute-done.1
  252.9 3.3 collective-permute-done
  256.2 0.2 convolution_convert_fusion
  256.5 0.1 reshape.54
  256.6 24.3 %all_to_all.21 = bf16[8,6,3584]{2,1,0:T(8,128)(2,1)S(1)} all-to-all(bf16[8,6,3584]{2,1,0:T(8,128)(2,1)S(1)} %reshape.54), channel_id=1, replica_groups={{0,8,16,24,32,40,48,56},{1,9,17,25,33,41,49,57},{2,10,18,26,34,42,50,58..., dimensions={0} | all-to-all | bytes 688128 | tf_op jit(solution)/shard_map/all_to_all | solution.py:90
  280.9 0.8 reshape.55
  281.7 0.0 all-gather.5.cloned.1.call-update
  281.8 0.0 reduce-scatter.5.cloned.1.call-start
  281.8 67.6 %all-gather.5.cloned.1.call-done = bf16[384,3584]{1,0:T(8,128)(2,1)} async-done(((bf16[48,3584]{1,0:T(8,128)(2,1)}), bf16[384,3584]{1,0:T(8,128)(2,1)}) %all-gather.5.cloned.1.call-update) | async-done | bytes 2752528 | tf_op jit(solution)/shard_map/all_gather | solution.py:98
  349.5 6.5 %conditional.5 = (bf16[384,3584]{1,0:T(8,128)(2,1)}) conditional(s32[]{:T(128)} %convert_element_type.62, (bf16[384,3584]{1,0:T(8,128)(2,1)}, bf16[192,3584]{1,0:T(8,128)(2,1)S(1)}, bf16[384,384]{1,0:T(8,128)(2,1)S(1)}, bf16[3584,384]{1,0:T(8,128)(2,1)}) %tuple.55, (bf16[384,3584]{1,0:T(8,128)(2,1)}, bf16[3584,384]{1,0:T(8,128)(2,1)}, ...), branch_computations={%region_5.6_spmd, %region_6.7_spmd} | conditional | flops 1587142656 | bytes 22118436
  349.5 0.2 copy.34
  349.7 0.0 copy-start.5
  349.7 3.0 fusion.25
  352.7 3.2 fusion.28
  355.9 0.0 reduce-scatter.5.cloned.1.call-update
  356.0 71.5 %reduce-scatter.5.cloned.1.call-done = bf16[48,3584]{1,0:T(8,128)(2,1)} async-done(((bf16[384,3584]{1,0:T(8,128)(2,1)}), bf16[48,3584]{1,0:T(8,128)(2,1)}) %reduce-scatter.5.cloned.1.call-update) | async-done | bytes 344080 | tf_op jit(solution)/shard_map/reduce_scatter | solution.py:102
  427.5 1.1 reshape.56
  428.6 45.4 %all_to_all.22 = bf16[8,6,3584]{2,1,0:T(8,128)(2,1)S(1)} all-to-all(bf16[8,6,3584]{2,1,0:T(8,128)(2,1)S(1)} %reshape.56), channel_id=1, replica_groups={{0,8,16,24,32,40,48,56},{1,9,17,25,33,41,49,57},{2,10,18,26,34,42,50,58..., dimensions={0} | all-to-all | bytes 688128 | tf_op jit(solution)/shard_map/all_to_all | solution.py:105
  474.0 0.1 reshape.57
  474.1 0.3 fusion.40
  474.4 0.8 maximum_bitcast_fusion
  (17 shorter events, 0.1 us)
Async XLA Ops:
  6.5 53.4 %copy-start.2 = (bf16[1,1,384,384]{3,2,1,0:T(8,128)(2,1)S(1)}, bf16[1,1,384,384]{3,2,1,0:T(8,128)(2,1)}, u32[]{:S(2)}) copy-start(bf16[1,1,384,384]{3,2,1,0:T(8,128)(2,1)} %param.11) | copy-start | bytes 884740
  6.5 117.1 %all-gather.3.cloned.1.call-start = ((), (), s32[]{:S(2)}) async-start(), calls=%async_computation.6 | async-start | bytes 3096576 | tf_op jit(solution)/shard_map/all_gather | solution.py:98
  8.1 115.5 %copy-start = (bf16[1,1,192,3584]{3,2,1,0:T(8,128)(2,1)S(1)}, bf16[1,1,192,3584]{3,2,1,0:T(8,128)(2,1)}, u32[]{:S(2)}) copy-start(bf16[1,1,192,3584]{3,2,1,0:T(8,128)(2,1)} %param.15) | copy-start | bytes 4128772
  59.9 142.0 %reduce-scatter.3.cloned.1.call-start = ((), (), s32[]{:S(2)}) async-start(), calls=%async_computation.7 | async-start | bytes 3096576 | tf_op jit(solution)/shard_map/reduce_scatter | solution.py:102
  130.4 86.3 %copy-start.3 = (f32[2,1,32,1]{2,3,1,0:T(1,128)S(1)}, f32[2,1,32,1]{2,3,1,0:T(1,128)}, u32[]{:S(2)}) copy-start(f32[2,1,32,1]{2,3,1,0:T(1,128)} %param.13) | copy-start | bytes 772
  130.4 119.2 %copy-start.1 = (bf16[1,32,3584]{2,1,0:T(8,128)(2,1)S(1)}, bf16[1,32,3584]{2,1,0:T(8,128)(2,1)}, u32[]{:S(2)}) copy-start(bf16[1,32,3584]{2,1,0:T(8,128)(2,1)} %param.10) | copy-start | bytes 688132
  203.7 45.7 %all-to-all-start.1 = ((bf16[8,6,3584]{2,1,0:T(8,128)(2,1)}), bf16[8,6,3584]{2,1,0:T(8,128)(2,1)S(1)}, u32[]{:S(2)}, u32[]{:S(2)}) async-start(bf16[8,6,3584]{2,1,0:T(8,128)(2,1)} %reshape.52), calls=%async_computation.2 | async-start | bytes 917504 | tf_op jit(solution)/shard_map/all_to_all | solution.py:105
  216.6 132.8 %all-gather.5.cloned.1.call-start = ((), (), s32[]{:S(2)}) async-start(), calls=%async_computation.8 | async-start | bytes 3096576 | tf_op jit(solution)/shard_map/all_gather | solution.py:98
  249.8 3.1 collective-permute-start.1
  251.6 4.6 collective-permute-start
  281.8 145.7 %reduce-scatter.5.cloned.1.call-start = ((), (), s32[]{:S(2)}) async-start(), calls=%async_computation.9 | async-start | bytes 3096576 | tf_op jit(solution)/shard_map/reduce_scatter | solution.py:102
  349.7 3.0 copy-start.5
Sparse Core Ops, SparseCore 0:
  60.0 63.5 all-gather.2
  130.5 71.2 reduce-scatter.2
  281.9 67.5 all-gather.4
  356.1 71.3 reduce-scatter.4

commit v2 on v1

--- a/solution.py
+++ b/solution.py
@@ -4,6 +4,8 @@
 from jax.sharding import PartitionSpec as P
 
 SHARDS = 8
+QUAD = 4
+MEETS = ((0, 1, 2, 3), (0, 1, 2, 3), (2, 3, 0, 1), (2, 3, 0, 1))
 
 
 def shifted(shard, axis, by):
@@ -53,24 +55,49 @@
     ).astype(jnp.bfloat16)
 
 
+def ring_of(first, size):
+    return [first + i for i in [*range(0, size, 2), *range(size - 1, 0, -2)]]
+
+
 def shards(entering, saved, routes, gates, w_in, w_out):
     peer_count = lax.axis_size("expert")
     experts = peer_count // SHARDS
+    quads = peer_count // QUAD
     tok_count = entering.shape[1]
     row_width = entering.shape[2]
     top_count = routes.shape[3]
     capacity = min(
         tok_count, max(2, (3 * tok_count * top_count + 2 * experts - 1) // (2 * experts))
     )
+    block_rows = quads * capacity
     w_in_dev = w_in[0, 0]
     w_out_dev = w_out[0, 0]
-    ring = list(range(0, SHARDS, 2)) + list(range(SHARDS - 1, 0, -2))
-    slice_groups = [[e * SHARDS + j for j in ring] for e in range(experts)]
-    expert_groups = [[e * SHARDS + j for e in range(experts)] for j in range(SHARDS)]
-    saved_dev = saved[0, 0].reshape(experts, SHARDS, capacity, -1)
-    saved_dev = jnp.stack([saved_dev[:, j] for j in ring]).reshape(peer_count * capacity, -1)
+    device_idx = lax.axis_index("expert")
+
+    meeting = [
+        [q * QUAD + MEETS[q % len(MEETS)][i] for q in range(quads)] for i in range(QUAD)
+    ]
+    group_of = {dev: i for i, group in enumerate(meeting) for dev in group}
+    rings = [ring_of(q * QUAD, QUAD) for q in range(quads)]
+    ring_pairs = [(ring[p], ring[(p + 1) % QUAD]) for ring in rings for p in range(QUAD)]
+    came_from = [[0] * QUAD for _ in range(peer_count)]
+    for ring in rings:
+        for p in range(QUAD):
+            came_from[ring[p]] = [group_of[ring[p - k]] for k in range(QUAD)]
+
+    saved_dev = saved[0, 0].reshape(peer_count, capacity, -1)
+    saved_groups = jnp.stack(
+        [jnp.concatenate([saved_dev[dev] for dev in group]) for group in meeting]
+    )
+    order = jnp.asarray(came_from, jnp.int32)[device_idx]
+    saved_blocks = jnp.concatenate(
+        [lax.dynamic_index_in_dim(saved_groups, order[k], keepdims=False) for k in range(QUAD)]
+    )
+
     section_idx = lax.axis_index("section")
+    sections = lax.axis_size("section")
     forward_first = section_idx % 2 == 0
+    partners = [(i, i ^ 1) for i in range(sections)]
     current = entering[0]
     collected = []
 
@@ -78,49 +105,51 @@
         return expert_forward(arrived_rows, w_in_dev, w_out_dev)
 
     def run_backward(arrived_rows):
-        return expert_backward(arrived_rows, saved_dev, w_in_dev, w_out_dev)
+        return expert_backward(arrived_rows, saved_blocks, w_in_dev, w_out_dev)
 
-    places = [routing_places(routes[t, 0], experts, capacity) for t in range(2)]
+    def meet(rows):
+        return lax.all_to_all(
+            rows.reshape(quads, capacity, row_width),
+            "expert",
+            split_axis=0,
+            concat_axis=0,
+            axis_index_groups=meeting,
+            tiled=True,
+        ).reshape(block_rows, row_width)
+
+    places = []
+    for tick_idx in range(2):
+        placed = routing_places(routes[tick_idx, 0], experts, capacity)
+        placed = placed.reshape(experts, 1, capacity, tok_count)
+        placed = jnp.broadcast_to(placed, (experts, SHARDS // QUAD, capacity, tok_count))
+        places.append(placed.reshape(block_rows, tok_count))
+
     for tick_idx in range(2):
         doing_forward = forward_first if tick_idx == 0 else jnp.logical_not(forward_first)
         placed = places[tick_idx]
         token_rows = jnp.dot(placed, current, preferred_element_type=jnp.float32).astype(
             jnp.bfloat16
         )
-        exchanged = lax.all_to_all(
-            token_rows.reshape(experts, capacity, row_width),
-            "expert",
-            split_axis=0,
-            concat_axis=0,
-            axis_index_groups=expert_groups,
-            tiled=True,
-        ).reshape(experts * capacity, row_width)
-        arrived = lax.all_gather(
-            exchanged, "expert", axis=0, axis_index_groups=slice_groups, tiled=True
-        )
-        expert_out = lax.cond(doing_forward, run_forward, run_backward, arrived)
-        summed = lax.psum_scatter(
-            expert_out, "expert", scatter_dimension=0, axis_index_groups=slice_groups, tiled=True
-        )
-        returned = lax.all_to_all(
-            summed.reshape(experts, capacity, row_width),
-            "expert",
-            split_axis=0,
-            concat_axis=0,
-            axis_index_groups=expert_groups,
-            tiled=True,
-        ).reshape(experts * capacity, row_width)
+        blocks = [meet(token_rows)]
+        for _ in range(QUAD - 1):
+            blocks.append(lax.ppermute(blocks[-1], "expert", ring_pairs))
+        expert_out = lax.cond(
+            doing_forward, run_forward, run_backward, jnp.concatenate(blocks)
+        ).reshape(QUAD, block_rows, row_width)
+        total = expert_out[1]
+        for step in range(1, QUAD):
+            got = lax.ppermute(total, "expert", ring_pairs).astype(jnp.float32)
+            own = expert_out[(step + 1) % QUAD].astype(jnp.float32)
+            total = (got + own).astype(jnp.bfloat16)
         picked = lax.dot_general(
-            placed, returned, (((0,), (0,)), ((), ())), preferred_element_type=jnp.float32
+            placed, meet(total), (((0,), (0,)), ((), ())), preferred_element_type=jnp.float32
         )
         layer_result = (
             current.astype(jnp.float32) + gates[tick_idx, 0, :, :] * picked
         ).astype(jnp.bfloat16)
         collected.append(layer_result)
         if tick_idx == 0:
-            from_below = shifted(layer_result, "section", 1)
-            from_above = shifted(layer_result, "section", -1)
-            current = jnp.where(forward_first, from_above, from_below)
+            current = lax.ppermute(layer_result, "section", partners)
     return jnp.stack(collected)[:, None]
 
 

time: 482 us -> 465 us (0.965)
  waiting for transfers between devices: 310 us -> 264 us
  starting transfers between devices: 16.1 us -> 44.8 us
  local copies, waits for them, and re-layouts: 6.4 us -> 23.5 us
  blocking collectives: 119 us -> 103 us
  between operations: 13.3 us -> 7.89 us
    ppermute x2 -> x13, waiting for transfers between devices: 3.3 us -> 174 us  [the longest x6 89.4 us: shards(): got = lax.ppermute(total, 'expert', ring_pairs).astype(jnp.float32)]
    reduce_scatter x2 -> x0, waiting for transfers between devices: 143 us -> none  [shards(): lax.psum_scatter(expert_out, 'expert', scatter_dimension=0, axis_index_gr...]
    all_gather x2 -> x0, waiting for transfers between devices: 131 us -> none  [shards(): lax.all_gather(exchanged, 'expert', axis=0, axis_index_groups=slice_group...]
    all_to_all x1 -> x2, waiting for transfers between devices: 32.7 us -> 90.1 us  [meet(): lax.all_to_all(rows.reshape(quads, capacity, row_width), 'expert', split_...]
    ppermute x2 -> x13, starting transfers between devices: 3.06 us -> 25.1 us  [the longest x6 11.7 us: shards(): blocks.append(lax.ppermute(blocks[-1], 'expert', ring_pairs))]
    all_to_all x3 -> x2, blocking collectives: 119 us -> 103 us  [meet(): lax.all_to_all(rows.reshape(quads, capacity, row_width), 'expert', split_...]
    unnamed x15 -> x30, local copies, waits for them, and re-layouts: 0.12 us -> 6.97 us
    all_to_all x1 -> x2, starting transfers between devices: 12.9 us -> 19.7 us  [meet(): lax.all_to_all(rows.reshape(quads, capacity, row_width), 'expert', split_...]
  transfers between devices with their start and end apart: 7 -> 15, of which waited for: 6 -> 15; matrix products, arithmetic and copies ran while one was open for 0% -> 3% of each run, Pallas kernels for 0% -> 0%
where the time goes in v2:
time: 465 us; the launch traced here: 464 us
  waiting for transfers between devices  264 us (57%)
  blocking collectives  103 us (22%)
  starting transfers between devices  44.8 us (10%)
  local copies, waits for them, and re-layouts  23.5 us (5%)
  matrix products  14.9 us (3%)
  between operations  7.89 us (2%)
  other arithmetic  5.16 us (1%)
    all_to_all x2, blocking collectives, meet(): lax.all_to_all(rows.reshape(quads, capacity, row_width), 'expert', split_...  103 us
    all_to_all x2, waiting for transfers between devices, meet(): lax.all_to_all(rows.reshape(quads, capacity, row_width), 'expert', split_...  90.1 us
    ppermute x6, waiting for transfers between devices, shards(): got = lax.ppermute(total, 'expert', ring_pairs).astype(jnp.float32)  89.4 us
    ppermute x6, waiting for transfers between devices, shards(): blocks.append(lax.ppermute(blocks[-1], 'expert', ring_pairs))  83.3 us
    all_to_all x2, starting transfers between devices, meet(): lax.all_to_all(rows.reshape(quads, capacity, row_width), 'expert', split_...  19.7 us
    ppermute x6, starting transfers between devices, shards(): blocks.append(lax.ppermute(blocks[-1], 'expert', ring_pairs))  11.7 us
    ppermute x6, starting transfers between devices, shards(): got = lax.ppermute(total, 'expert', ring_pairs).astype(jnp.float32)  11.5 us
  transfers between devices with their start and end apart: 15, of which 15 were waited for; matrix products, arithmetic and copies ran while one was open for 3% of the time, Pallas kernels for 0%

profile of v2, /device:TPU:32, one launch (start us, length us, event | category | flops | bytes accessed | tf_op | source)
XLA Modules:
  0.0 463.9 jit_solution(15511871934455982927)
XLA Ops:
  1.7 1.2 convolution_convert_fusion.1
  3.0 1.2 reshape.239
  4.1 16.0 %all-to-all-start = ((bf16[16,6,3584]{2,1,0:T(8,128)(2,1)}), bf16[16,6,3584]{2,1,0:T(8,128)(2,1)S(1)}, u32[]{:S(2)}, u32[]{:S(2)}) async-start(bf16[16,6,3584]{2,1,0:T(8,128)(2,1)} %reshape.239), calls=%async_computation | async-start | bytes 1835008 | tf_op jit(solution)/shard_map/all_to_all | solution.py:111
  21.0 48.6 %all-to-all-done = bf16[16,6,3584]{2,1,0:T(8,128)(2,1)S(1)} async-done(((bf16[16,6,3584]{2,1,0:T(8,128)(2,1)}), bf16[16,6,3584]{2,1,0:T(8,128)(2,1)S(1)}, u32[]{:S(2)}, u32[]{:S(2)}) %all-to-all-start) | async-done | bytes 688160 | tf_op jit(solution)/shard_map/all_to_all | solution.py:111
  69.8 1.9 collective-permute-start
  82.0 1.0 concatenate.30
  84.1 5.4 %collective-permute-done = bf16[96,3584]{1,0:T(8,128)(2,1)S(1)} collective-permute-done((bf16[96,3584]{1,0:T(8,128)(2,1)S(1)}, bf16[96,3584]{1,0:T(8,128)(2,1)S(1)}, u32[]{:S(2)}, u32[]{:S(2)}) %collective-permute-start) | collective-permute-done | bytes 688160 | tf_op jit(solution)/shard_map/ppermute | solution.py:135
  89.5 1.9 collective-permute-start.1
  93.1 15.2 %collective-permute-done.1 = bf16[96,3584]{1,0:T(8,128)(2,1)S(1)} collective-permute-done((bf16[96,3584]{1,0:T(8,128)(2,1)S(1)}, bf16[96,3584]{1,0:T(8,128)(2,1)S(1)}, u32[]{:S(2)}, u32[]{:S(2)}) %collective-permute-start.1) | collective-permute-done | bytes 688160 | tf_op jit(solution)/shard_map/ppermute | solution.py:135
  108.3 1.9 collective-permute-start.2
  112.1 14.2 %collective-permute-done.2 = bf16[96,3584]{1,0:T(8,128)(2,1)S(1)} collective-permute-done((bf16[96,3584]{1,0:T(8,128)(2,1)S(1)}, bf16[96,3584]{1,0:T(8,128)(2,1)S(1)}, u32[]{:S(2)}, u32[]{:S(2)}) %collective-permute-start.2) | collective-permute-done | bytes 688160 | tf_op jit(solution)/shard_map/ppermute | solution.py:135
  127.2 8.3 %conditional.4 = (bf16[384,3584]{1,0:T(8,128)(2,1)}) conditional(s32[]{:T(128)} %convert_element_type.124, (bf16[384,3584]{1,0:T(8,128)(2,1)}, bf16[192,3584]{1,0:T(8,128)(2,1)S(1)}, bf16[384,384]{0,1:T(8,128)(2,1)S(1)}, bf16[3584,384]{1,0:T(8,128)(2,1)S(1)}) %tuple.109, (bf16[384,3584]{1,0:T(8,128)(2,1)}, bf16[3584,384]{1,0:T(8,128)(2,1)S(1)}, ...), branch_computations={%region_1.2_spmd, %region_2.3_spmd} | conditional | flops 1587142656 | bytes 21823524
  127.2 1.6 copy-done.12
  128.8 4.2 fusion.45
  133.0 2.5 fusion.15
  135.5 1.3 slice.424
  136.8 1.9 collective-permute-start.3
  138.8 13.0 %collective-permute-done.3 = bf16[96,3584]{1,0:T(8,128)(2,1)S(1)} collective-permute-done((bf16[96,3584]{1,0:T(8,128)(2,1)S(1)}, bf16[96,3584]{1,0:T(8,128)(2,1)S(1)}, u32[]{:S(2)}, u32[]{:S(2)}) %collective-permute-start.3) | collective-permute-done | bytes 688160 | tf_op jit(solution)/shard_map/ppermute | solution.py:141
  151.7 1.3 add_convert_fusion.5
  153.0 1.9 collective-permute-start.4
  154.9 13.5 %collective-permute-done.4 = bf16[96,3584]{1,0:T(8,128)(2,1)S(1)} collective-permute-done((bf16[96,3584]{1,0:T(8,128)(2,1)S(1)}, bf16[96,3584]{1,0:T(8,128)(2,1)S(1)}, u32[]{:S(2)}, u32[]{:S(2)}) %collective-permute-start.4) | collective-permute-done | bytes 688160 | tf_op jit(solution)/shard_map/ppermute | solution.py:141
  168.6 1.9 collective-permute-start.5
  170.5 11.8 %collective-permute-done.5 = bf16[96,3584]{1,0:T(8,128)(2,1)S(1)} collective-permute-done((bf16[96,3584]{1,0:T(8,128)(2,1)S(1)}, bf16[96,3584]{1,0:T(8,128)(2,1)S(1)}, u32[]{:S(2)}, u32[]{:S(2)}) %collective-permute-start.5) | collective-permute-done | bytes 688160 | tf_op jit(solution)/shard_map/ppermute | solution.py:141
  182.5 1.2 reshape.241
  183.7 3.6 all-to-all-start.1
  187.3 41.5 %all-to-all-done.1 = bf16[16,6,3584]{2,1,0:T(8,128)(2,1)S(1)} async-done(((bf16[16,6,3584]{2,1,0:T(8,128)(2,1)}), bf16[16,6,3584]{2,1,0:T(8,128)(2,1)S(1)}, u32[]{:S(2)}, u32[]{:S(2)}) %all-to-all-start.1) | async-done | bytes 688160 | tf_op jit(solution)/shard_map/all_to_all | solution.py:111
  229.3 1.9 collective-permute-start.6
  231.3 1.4 collective-permute-done.6
  233.6 53.2 %all_to_all.20 = bf16[16,6,3584]{2,1,0:T(8,128)(2,1)S(1)} all-to-all(bf16[16,6,3584]{2,1,0:T(8,128)(2,1)S(1)} %reshape.244), channel_id=1, replica_groups={{0,4,10,14,16,20,26,30,32,36,42,46,48,52,58,62},{1,5,11,15,17,21,27,31,..., dimensions={0} | all-to-all | bytes 1376256 | tf_op jit(solution)/shard_map/all_to_all | solution.py:111
  287.0 2.1 collective-permute-start.7
  289.1 18.1 %collective-permute-done.7 = bf16[96,3584]{1,0:T(8,128)(2,1)S(1)} collective-permute-done((bf16[96,3584]{1,0:T(8,128)(2,1)S(1)}, bf16[96,3584]{1,0:T(8,128)(2,1)S(1)}, u32[]{:S(2)}, u32[]{:S(2)}) %collective-permute-start.7) | collective-permute-done | bytes 688160 | tf_op jit(solution)/shard_map/ppermute | solution.py:135
  307.2 1.9 collective-permute-start.8
  310.1 16.6 %collective-permute-done.8 = bf16[96,3584]{1,0:T(8,128)(2,1)} collective-permute-done((bf16[96,3584]{1,0:T(8,128)(2,1)S(1)}, bf16[96,3584]{1,0:T(8,128)(2,1)}, u32[]{:S(2)}, u32[]{:S(2)}) %collective-permute-start.8) | collective-permute-done | bytes 688160 | tf_op jit(solution)/shard_map/ppermute | solution.py:135
  326.6 1.9 collective-permute-start.9
  329.4 2.0 constant_dynamic-update-slice_fusion.5
  331.4 13.8 %collective-permute-done.9 = bf16[96,3584]{1,0:T(8,128)(2,1)S(1)} collective-permute-done((bf16[96,3584]{1,0:T(8,128)(2,1)}, bf16[96,3584]{1,0:T(8,128)(2,1)S(1)}, u32[]{:S(2)}, u32[]{:S(2)}) %collective-permute-start.9) | collective-permute-done | bytes 688160 | tf_op jit(solution)/shard_map/ppermute | solution.py:135
  346.2 6.1 %conditional.5 = (bf16[384,3584]{1,0:T(8,128)(2,1)}) conditional(s32[]{:T(128)} %convert_element_type.139, (bf16[384,3584]{1,0:T(8,128)(2,1)}, bf16[192,3584]{1,0:T(8,128)(2,1)S(1)}, bf16[384,384]{0,1:T(8,128)(2,1)S(1)}, bf16[3584,384]{1,0:T(8,128)(2,1)S(1)}) %tuple.111, (bf16[384,3584]{1,0:T(8,128)(2,1)}, bf16[3584,384]{1,0:T(8,128)(2,1)S(1)}, ...), branch_computations={%region_4.5_spmd, %region_5.6_spmd} | conditional | flops 1587142656 | bytes 21823524
  346.2 2.9 fusion.25
  349.0 3.2 fusion.28
  352.2 1.3 slice.428
  353.5 1.9 collective-permute-start.10
  355.5 17.9 %collective-permute-done.10 = bf16[96,3584]{1,0:T(8,128)(2,1)S(1)} collective-permute-done((bf16[96,3584]{1,0:T(8,128)(2,1)S(1)}, bf16[96,3584]{1,0:T(8,128)(2,1)S(1)}, u32[]{:S(2)}, u32[]{:S(2)}) %collective-permute-start.10) | collective-permute-done | bytes 688160 | tf_op jit(solution)/shard_map/ppermute | solution.py:141
  373.4 1.3 add_convert_fusion.2
  374.6 1.9 collective-permute-start.11
  376.6 17.0 %collective-permute-done.11 = bf16[96,3584]{1,0:T(8,128)(2,1)S(1)} collective-permute-done((bf16[96,3584]{1,0:T(8,128)(2,1)S(1)}, bf16[96,3584]{1,0:T(8,128)(2,1)S(1)}, u32[]{:S(2)}, u32[]{:S(2)}) %collective-permute-start.11) | collective-permute-done | bytes 688160 | tf_op jit(solution)/shard_map/ppermute | solution.py:141
  393.8 1.9 collective-permute-start.12
  395.7 16.2 %collective-permute-done.12 = bf16[96,3584]{1,0:T(8,128)(2,1)S(1)} collective-permute-done((bf16[96,3584]{1,0:T(8,128)(2,1)S(1)}, bf16[96,3584]{1,0:T(8,128)(2,1)S(1)}, u32[]{:S(2)}, u32[]{:S(2)}) %collective-permute-start.12) | collective-permute-done | bytes 688160 | tf_op jit(solution)/shard_map/ppermute | solution.py:141
  412.3 50.3 %all_to_all.21 = bf16[16,6,3584]{2,1,0:T(8,128)(2,1)S(1)} all-to-all(bf16[16,6,3584]{2,1,0:T(8,128)(2,1)S(1)} %reshape.246), channel_id=1, replica_groups={{0,4,10,14,16,20,26,30,32,36,42,46,48,52,58,62},{1,5,11,15,17,21,27,31,..., dimensions={0} | all-to-all | bytes 1376256 | tf_op jit(solution)/shard_map/all_to_all | solution.py:111
  (72 shorter events, 17.5 us)
Async XLA Ops:
  0.0 20.9 %copy-start.6 = (bf16[1,1,384,384]{3,2,1,0:T(8,128)(2,1)S(1)}, bf16[1,1,384,384]{3,2,1,0:T(8,128)(2,1)}, u32[]{:S(2)}) copy-start(bf16[1,1,384,384]{3,2,1,0:T(8,128)(2,1)} %param.12) | copy-start | bytes 884740
  4.1 65.4 %all-to-all-start = ((bf16[16,6,3584]{2,1,0:T(8,128)(2,1)}), bf16[16,6,3584]{2,1,0:T(8,128)(2,1)S(1)}, u32[]{:S(2)}, u32[]{:S(2)}) async-start(bf16[16,6,3584]{2,1,0:T(8,128)(2,1)} %reshape.239), calls=%async_computation | async-start | bytes 1835008 | tf_op jit(solution)/shard_map/all_to_all | solution.py:111
  69.8 19.7 %collective-permute-start = (bf16[96,3584]{1,0:T(8,128)(2,1)S(1)}, bf16[96,3584]{1,0:T(8,128)(2,1)S(1)}, u32[]{:S(2)}, u32[]{:S(2)}) collective-permute-start(bf16[96,3584]{1,0:T(8,128)(2,1)S(1)} %reshape.240), channel_id=1, source_target_pairs={{0,2},{2,3},{3,1},{1,0},{4,6},{6,7},{7,5},{5,4},{8,10},{10,11},{11... | collective-permute-start | bytes 2064392 | tf_op jit(solution)/shard_map/ppermute | solution.py:135
  89.5 18.8 %collective-permute-start.1 = (bf16[96,3584]{1,0:T(8,128)(2,1)S(1)}, bf16[96,3584]{1,0:T(8,128)(2,1)S(1)}, u32[]{:S(2)}, u32[]{:S(2)}) collective-permute-start(bf16[96,3584]{1,0:T(8,128)(2,1)S(1)} %collective-permute-done), channel_id=1, source_target_pairs={{0,2},{2,3},{3,1},{1,0},{4,6},{6,7},{7,5},{5,4},{8,10},{10,11},{11... | collective-permute-start | bytes 2064392 | tf_op jit(solution)/shard_map/ppermute | solution.py:135
  92.2 35.0 %copy-start.7 = (bf16[384,384]{0,1:T(8,128)(2,1)}, bf16[384,384]{0,1:T(8,128)(2,1)S(1)}, u32[]{:S(2)}) copy-start(bf16[384,384]{0,1:T(8,128)(2,1)S(1)} %pad_maximum_fusion.1) | copy-start | bytes 884740
  92.2 35.0 %copy-start = (bf16[1,1,192,3584]{3,2,1,0:T(8,128)(2,1)S(1)}, bf16[1,1,192,3584]{3,2,1,0:T(8,128)(2,1)}, u32[]{:S(2)}) copy-start(bf16[1,1,192,3584]{3,2,1,0:T(8,128)(2,1)} %param.16) | copy-start | bytes 4128772
  92.2 35.0 %copy-start.10 = (bf16[1,1,3584,384]{3,2,1,0:T(8,128)(2,1)S(1)}, bf16[1,1,3584,384]{3,2,1,0:T(8,128)(2,1)}, u32[]{:S(2)}) copy-start(bf16[1,1,3584,384]{3,2,1,0:T(8,128)(2,1)} %param.15) | copy-start | bytes 8257540
  108.3 18.0 %collective-permute-start.2 = (bf16[96,3584]{1,0:T(8,128)(2,1)S(1)}, bf16[96,3584]{1,0:T(8,128)(2,1)S(1)}, u32[]{:S(2)}, u32[]{:S(2)}) collective-permute-start(bf16[96,3584]{1,0:T(8,128)(2,1)S(1)} %collective-permute-done.1), channel_id=1, source_target_pairs={{0,2},{2,3},{3,1},{1,0},{4,6},{6,7},{7,5},{5,4},{8,10},{10,11},{11... | collective-permute-start | bytes 2064392 | tf_op jit(solution)/shard_map/ppermute | solution.py:135
  127.2 1.6 copy-start.12
  135.5 32.9 %copy-start.1 = (bf16[384,3584]{1,0:T(8,128)(2,1)S(1)}, bf16[384,3584]{1,0:T(8,128)(2,1)}, u32[]{:S(2)}) copy-start(bf16[384,3584]{1,0:T(8,128)(2,1)} %get-tuple-element.143) | copy-start | bytes 8257540
  136.8 14.9 %collective-permute-start.3 = (bf16[96,3584]{1,0:T(8,128)(2,1)S(1)}, bf16[96,3584]{1,0:T(8,128)(2,1)S(1)}, u32[]{:S(2)}, u32[]{:S(2)}) collective-permute-start(bf16[96,3584]{1,0:T(8,128)(2,1)S(1)} %slice.424), channel_id=1, source_target_pairs={{0,2},{2,3},{3,1},{1,0},{4,6},{6,7},{7,5},{5,4},{8,10},{10,11},{11... | collective-permute-start | bytes 2064392 | tf_op jit(solution)/shard_map/ppermute | solution.py:141
  153.0 15.4 %collective-permute-start.4 = (bf16[96,3584]{1,0:T(8,128)(2,1)S(1)}, bf16[96,3584]{1,0:T(8,128)(2,1)S(1)}, u32[]{:S(2)}, u32[]{:S(2)}) collective-permute-start(bf16[96,3584]{1,0:T(8,128)(2,1)S(1)} %add_convert_fusion.5), channel_id=1, source_target_pairs={{0,2},{2,3},{3,1},{1,0},{4,6},{6,7},{7,5},{5,4},{8,10},{10,11},{11... | collective-permute-start | bytes 2064392 | tf_op jit(solution)/shard_map/ppermute | solution.py:141
  168.6 18.7 %copy-start.9 = (f32[2,1,32,1]{2,3,1,0:T(1,128)S(1)}, f32[2,1,32,1]{2,3,1,0:T(1,128)}, u32[]{:S(2)}) copy-start(f32[2,1,32,1]{2,3,1,0:T(1,128)} %param.14) | copy-start | bytes 772
  168.6 13.7 %collective-permute-start.5 = (bf16[96,3584]{1,0:T(8,128)(2,1)S(1)}, bf16[96,3584]{1,0:T(8,128)(2,1)S(1)}, u32[]{:S(2)}, u32[]{:S(2)}) collective-permute-start(bf16[96,3584]{1,0:T(8,128)(2,1)S(1)} %add_convert_fusion.4), channel_id=1, source_target_pairs={{0,2},{2,3},{3,1},{1,0},{4,6},{6,7},{7,5},{5,4},{8,10},{10,11},{11... | collective-permute-start | bytes 2064392 | tf_op jit(solution)/shard_map/ppermute | solution.py:141
  182.5 46.5 %copy-start.3 = (bf16[1,32,3584]{2,1,0:T(8,128)(2,1)S(1)}, bf16[1,32,3584]{2,1,0:T(8,128)(2,1)}, u32[]{:S(2)}) copy-start(bf16[1,32,3584]{2,1,0:T(8,128)(2,1)} %param.11) | copy-start | bytes 688132
  183.7 45.1 %all-to-all-start.1 = ((bf16[16,6,3584]{2,1,0:T(8,128)(2,1)}), bf16[16,6,3584]{2,1,0:T(8,128)(2,1)S(1)}, u32[]{:S(2)}, u32[]{:S(2)}) async-start(bf16[16,6,3584]{2,1,0:T(8,128)(2,1)} %reshape.241), calls=%async_computation.1 | async-start | bytes 1835008 | tf_op jit(solution)/shard_map/all_to_all | solution.py:111
  229.3 3.4 collective-permute-start.6
  232.7 0.7 copy-start.4
  287.0 20.2 %collective-permute-start.7 = (bf16[96,3584]{1,0:T(8,128)(2,1)S(1)}, bf16[96,3584]{1,0:T(8,128)(2,1)S(1)}, u32[]{:S(2)}, u32[]{:S(2)}) collective-permute-start(bf16[96,3584]{1,0:T(8,128)(2,1)S(1)} %reshape.245), channel_id=1, source_target_pairs={{0,2},{2,3},{3,1},{1,0},{4,6},{6,7},{7,5},{5,4},{8,10},{10,11},{11... | collective-permute-start | bytes 2064392 | tf_op jit(solution)/shard_map/ppermute | solution.py:135
  307.2 19.4 %collective-permute-start.8 = (bf16[96,3584]{1,0:T(8,128)(2,1)S(1)}, bf16[96,3584]{1,0:T(8,128)(2,1)}, u32[]{:S(2)}, u32[]{:S(2)}) collective-permute-start(bf16[96,3584]{1,0:T(8,128)(2,1)S(1)} %collective-permute-done.7), channel_id=1, source_target_pairs={{0,2},{2,3},{3,1},{1,0},{4,6},{6,7},{7,5},{5,4},{8,10},{10,11},{11... | collective-permute-start | bytes 2064392 | tf_op jit(solution)/shard_map/ppermute | solution.py:135
  309.1 37.0 %copy-start.8 = (bf16[384,384]{0,1:T(8,128)(2,1)S(1)}, bf16[384,384]{0,1:T(8,128)(2,1)}, u32[]{:S(2)}) copy-start(bf16[384,384]{0,1:T(8,128)(2,1)} %copy-done.7) | copy-start | bytes 884740
  309.1 37.0 %copy-start.11 = (bf16[1,1,3584,384]{3,2,1,0:T(8,128)(2,1)S(1)}, bf16[1,1,3584,384]{3,2,1,0:T(8,128)(2,1)}, u32[]{:S(2)}) copy-start(bf16[1,1,3584,384]{3,2,1,0:T(8,128)(2,1)} %param.15) | copy-start | bytes 8257540
  326.6 18.7 %collective-permute-start.9 = (bf16[96,3584]{1,0:T(8,128)(2,1)}, bf16[96,3584]{1,0:T(8,128)(2,1)S(1)}, u32[]{:S(2)}, u32[]{:S(2)}) collective-permute-start(bf16[96,3584]{1,0:T(8,128)(2,1)} %collective-permute-done.8), channel_id=1, source_target_pairs={{0,2},{2,3},{3,1},{1,0},{4,6},{6,7},{7,5},{5,4},{8,10},{10,11},{11... | collective-permute-start | bytes 2064392 | tf_op jit(solution)/shard_map/ppermute | solution.py:135
  352.2 41.3 %copy-start.2 = (bf16[384,3584]{1,0:T(8,128)(2,1)S(1)}, bf16[384,3584]{1,0:T(8,128)(2,1)}, u32[]{:S(2)}) copy-start(bf16[384,3584]{1,0:T(8,128)(2,1)} %get-tuple-element.144) | copy-start | bytes 8257540
  353.5 19.8 %collective-permute-start.10 = (bf16[96,3584]{1,0:T(8,128)(2,1)S(1)}, bf16[96,3584]{1,0:T(8,128)(2,1)S(1)}, u32[]{:S(2)}, u32[]{:S(2)}) collective-permute-start(bf16[96,3584]{1,0:T(8,128)(2,1)S(1)} %slice.428), channel_id=1, source_target_pairs={{0,2},{2,3},{3,1},{1,0},{4,6},{6,7},{7,5},{5,4},{8,10},{10,11},{11... | collective-permute-start | bytes 2064392 | tf_op jit(solution)/shard_map/ppermute | solution.py:141
  374.6 19.0 %collective-permute-start.11 = (bf16[96,3584]{1,0:T(8,128)(2,1)S(1)}, bf16[96,3584]{1,0:T(8,128)(2,1)S(1)}, u32[]{:S(2)}, u32[]{:S(2)}) collective-permute-start(bf16[96,3584]{1,0:T(8,128)(2,1)S(1)} %add_convert_fusion.2), channel_id=1, source_target_pairs={{0,2},{2,3},{3,1},{1,0},{4,6},{6,7},{7,5},{5,4},{8,10},{10,11},{11... | collective-permute-start | bytes 2064392 | tf_op jit(solution)/shard_map/ppermute | solution.py:141
  393.8 18.1 %collective-permute-start.12 = (bf16[96,3584]{1,0:T(8,128)(2,1)S(1)}, bf16[96,3584]{1,0:T(8,128)(2,1)S(1)}, u32[]{:S(2)}, u32[]{:S(2)}) collective-permute-start(bf16[96,3584]{1,0:T(8,128)(2,1)S(1)} %add_convert_fusion.1), channel_id=1, source_target_pairs={{0,2},{2,3},{3,1},{1,0},{4,6},{6,7},{7,5},{5,4},{8,10},{10,11},{11... | collective-permute-start | bytes 2064392 | tf_op jit(solution)/shard_map/ppermute | solution.py:141
  412.0 50.8 %copy-start.5 = (bf16[32,3584]{1,0:T(8,128)(2,1)S(1)}, bf16[32,3584]{1,0:T(8,128)(2,1)}, u32[]{:S(2)}) copy-start(bf16[32,3584]{1,0:T(8,128)(2,1)} %copy-done.4) | copy-start | bytes 688132

commit v3 on v2

--- a/solution.py
+++ b/solution.py
@@ -4,8 +4,8 @@
 from jax.sharding import PartitionSpec as P
 
 SHARDS = 8
-QUAD = 4
-MEETS = ((0, 1, 2, 3), (0, 1, 2, 3), (2, 3, 0, 1), (2, 3, 0, 1))
+QUAD = 8
+MEETS = ((0, 1, 2, 3, 4, 5, 6, 7), (7, 6, 5, 4, 3, 2, 1, 0))
 
 
 def shifted(shard, axis, by):
@@ -85,14 +85,17 @@
         for p in range(QUAD):
             came_from[ring[p]] = [group_of[ring[p - k]] for k in range(QUAD)]
 
-    saved_dev = saved[0, 0].reshape(peer_count, capacity, -1)
-    saved_groups = jnp.stack(
-        [jnp.concatenate([saved_dev[dev] for dev in group]) for group in meeting]
+    rows_of = [
+        [dev * capacity + c for dev in group for c in range(capacity)] for group in meeting
+    ]
+    wanted = [[row for i in came for row in rows_of[i]] for came in came_from]
+    wanted = lax.dynamic_index_in_dim(
+        jnp.asarray(wanted, jnp.int32), device_idx, keepdims=False
     )
-    order = jnp.asarray(came_from, jnp.int32)[device_idx]
-    saved_blocks = jnp.concatenate(
-        [lax.dynamic_index_in_dim(saved_groups, order[k], keepdims=False) for k in range(QUAD)]
-    )
+    row_ids = jnp.arange(peer_count * capacity, dtype=jnp.int32)
+    picking = (wanted[:, None] == row_ids[None, :]).astype(jnp.bfloat16)
+    saved_blocks = jnp.dot(picking, saved[0, 0], preferred_element_type=jnp.float32)
+    saved_blocks = jnp.split(saved_blocks.astype(jnp.bfloat16), QUAD)
 
     section_idx = lax.axis_index("section")
     sections = lax.axis_size("section")
@@ -101,15 +104,19 @@
     current = entering[0]
     collected = []
 
-    def run_forward(arrived_rows):
-        return expert_forward(arrived_rows, w_in_dev, w_out_dev)
+    def run_expert(rows, saved_rows, doing_forward):
+        return lax.cond(
+            doing_forward,
+            lambda: expert_forward(rows, w_in_dev, w_out_dev),
+            lambda: expert_backward(rows, saved_rows, w_in_dev, w_out_dev),
+        )
 
-    def run_backward(arrived_rows):
-        return expert_backward(arrived_rows, saved_blocks, w_in_dev, w_out_dev)
+    def added(left, right):
+        return (left.astype(jnp.float32) + right.astype(jnp.float32)).astype(jnp.bfloat16)
 
     def meet(rows):
         return lax.all_to_all(
-            rows.reshape(quads, capacity, row_width),
+            rows.reshape(quads, capacity // 2, 2, row_width),
             "expert",
             split_axis=0,
             concat_axis=0,
@@ -130,17 +137,15 @@
         token_rows = jnp.dot(placed, current, preferred_element_type=jnp.float32).astype(
             jnp.bfloat16
         )
-        blocks = [meet(token_rows)]
-        for _ in range(QUAD - 1):
-            blocks.append(lax.ppermute(blocks[-1], "expert", ring_pairs))
-        expert_out = lax.cond(
-            doing_forward, run_forward, run_backward, jnp.concatenate(blocks)
-        ).reshape(QUAD, block_rows, row_width)
-        total = expert_out[1]
+        block = meet(token_rows)
+        own = run_expert(block, saved_blocks[0], doing_forward)
+        total = None
         for step in range(1, QUAD):
-            got = lax.ppermute(total, "expert", ring_pairs).astype(jnp.float32)
-            own = expert_out[(step + 1) % QUAD].astype(jnp.float32)
-            total = (got + own).astype(jnp.bfloat16)
+            block = lax.ppermute(block, "expert", ring_pairs)
+            result = run_expert(block, saved_blocks[step], doing_forward)
+            total = result if total is None else added(total, result)
+            total = lax.ppermute(total, "expert", ring_pairs)
+        total = added(total, own)
         picked = lax.dot_general(
             placed, meet(total), (((0,), (0,)), ((), ())), preferred_element_type=jnp.float32
         )

time: 465 us -> 369 us (0.79)
  the two profiles are of different devices: /device:TPU:32 before, /device:TPU:70 now
where the time goes in v3:
time: 369 us; the launch traced here: 367 us
  starting transfers between devices  153 us (41%)
  waiting for transfers between devices  76.5 us (21%)
  matrix products  56.5 us (15%)
  blocking collectives  40.3 us (11%)
  other arithmetic  27.9 us (8%)
  local copies, waits for them, and re-layouts  11.5 us (3%)
    ppermute x14, starting transfers between devices, shards(): block = lax.ppermute(block, 'expert', ring_pairs)  79.9 us
    ppermute x14, starting transfers between devices, shards(): total = lax.ppermute(total, 'expert', ring_pairs)  54.5 us
    all_to_all x2, blocking collectives, meet(): lax.all_to_all(rows.reshape(quads, capacity // 2, 2, row_width), 'expert'...  40.3 us
    ppermute x14, waiting for transfers between devices, shards(): block = lax.ppermute(block, 'expert', ring_pairs)  39.5 us
    all_to_all x2, waiting for transfers between devices, meet(): lax.all_to_all(rows.reshape(quads, capacity // 2, 2, row_width), 'expert'...  28.1 us
    convert_element_type x14, other arithmetic, added(): (left.astype(jnp.float32) + right.astype(jnp.float32)).astype(jnp.bfloat16)  26.2 us
    all_to_all x2, starting transfers between devices, meet(): lax.all_to_all(rows.reshape(quads, capacity // 2, 2, row_width), 'expert'...  17.1 us
    dot_general x8, matrix products, expert_backward(): lax.dot_general(grad_rows, w_out_dev, (((1,), (1,)), ((), ())), preferred...  15.5 us
  transfers between devices with their start and end apart: 31, of which 17 were waited for; matrix products, arithmetic and copies ran while one was open for 21% of the time, Pallas kernels for 0%

profile of v3, /device:TPU:70, one launch (start us, length us, event | category | flops | bytes accessed | tf_op | source)
XLA Modules:
  0.0 367.2 jit_solution(14744058913382988601)
XLA Ops:
  3.7 13.4 %all-to-all-start = ((bf16[8,3,2,3584]{3,2,1,0:T(2,128)(2,1)}), bf16[8,3,2,3584]{3,2,1,0:T(2,128)(2,1)}, u32[]{:S(2)}, u32[]{:S(2)}) async-start(bf16[8,3,2,3584]{3,2,1,0:T(2,128)(2,1)} %reshape.48), calls=%async_computation | async-start | bytes 688128 | tf_op jit(solution)/shard_map/all_to_all | solution.py:118
  17.8 16.2 %all-to-all-done = bf16[8,3,2,3584]{3,2,1,0:T(2,128)(2,1)} async-done(((bf16[8,3,2,3584]{3,2,1,0:T(2,128)(2,1)}), bf16[8,3,2,3584]{3,2,1,0:T(2,128)(2,1)}, u32[]{:S(2)}, u32[]{:S(2)}) %all-to-all-start) | async-done | bytes 344096 | tf_op jit(solution)/shard_map/all_to_all | solution.py:118
  35.1 3.6 collective-permute-start
  41.4 5.2 %collective-permute-done = bf16[48,3584]{1,0:T(8,128)(2,1)} collective-permute-done((bf16[48,3584]{1,0:T(8,128)(2,1)S(1)}, bf16[48,3584]{1,0:T(8,128)(2,1)}, u32[]{:S(2)}, u32[]{:S(2)}) %collective-permute-start) | collective-permute-done | bytes 344096 | tf_op jit(solution)/shard_map/ppermute | solution.py:144
  46.6 4.7 %collective-permute-start.2 = (bf16[48,3584]{1,0:T(8,128)(2,1)}, bf16[48,3584]{1,0:T(8,128)(2,1)}, u32[]{:S(2)}, u32[]{:S(2)}) collective-permute-start(bf16[48,3584]{1,0:T(8,128)(2,1)} %collective-permute-done), channel_id=1, source_target_pairs={{0,2},{2,4},{4,6},{6,7},{7,5},{5,3},{3,1},{1,0},{8,10},{10,12},{12... | collective-permute-start | bytes 1032200 | tf_op jit(solution)/shard_map/ppermute | solution.py:144
  54.1 2.9 collective-permute-start.1
  61.2 6.5 %collective-permute-start.4 = (bf16[48,3584]{1,0:T(8,128)(2,1)}, bf16[48,3584]{1,0:T(8,128)(2,1)}, u32[]{:S(2)}, u32[]{:S(2)}) collective-permute-start(bf16[48,3584]{1,0:T(8,128)(2,1)} %collective-permute-done.2), channel_id=1, source_target_pairs={{0,2},{2,4},{4,6},{6,7},{7,5},{5,3},{3,1},{1,0},{8,10},{10,12},{12... | collective-permute-start | bytes 1032200 | tf_op jit(solution)/shard_map/ppermute | solution.py:144
  74.5 2.9 conditional.26
  77.4 6.3 %collective-permute-start.6 = (bf16[48,3584]{1,0:T(8,128)(2,1)}, bf16[48,3584]{1,0:T(8,128)(2,1)}, u32[]{:S(2)}, u32[]{:S(2)}) collective-permute-start(bf16[48,3584]{1,0:T(8,128)(2,1)} %collective-permute-done.4), channel_id=1, source_target_pairs={{0,2},{2,4},{4,6},{6,7},{7,5},{5,3},{3,1},{1,0},{8,10},{10,12},{12... | collective-permute-start | bytes 1032200 | tf_op jit(solution)/shard_map/ppermute | solution.py:144
  85.7 4.5 %collective-permute-start.5 = (bf16[48,3584]{1,0:T(8,128)(2,1)}, bf16[48,3584]{1,0:T(8,128)(2,1)}, u32[]{:S(2)}, u32[]{:S(2)}) collective-permute-start(bf16[48,3584]{1,0:T(8,128)(2,1)} %add_convert_fusion.12), channel_id=1, source_target_pairs={{0,2},{2,4},{4,6},{6,7},{7,5},{5,3},{3,1},{1,0},{8,10},{10,12},{12... | collective-permute-start | bytes 1032200 | tf_op jit(solution)/shard_map/ppermute | solution.py:147
  90.2 2.9 conditional.27
  93.1 6.1 %collective-permute-start.8 = (bf16[48,3584]{1,0:T(8,128)(2,1)}, bf16[48,3584]{1,0:T(8,128)(2,1)}, u32[]{:S(2)}, u32[]{:S(2)}) collective-permute-start(bf16[48,3584]{1,0:T(8,128)(2,1)} %collective-permute-done.6), channel_id=1, source_target_pairs={{0,2},{2,4},{4,6},{6,7},{7,5},{5,3},{3,1},{1,0},{8,10},{10,12},{12... | collective-permute-start | bytes 1032200 | tf_op jit(solution)/shard_map/ppermute | solution.py:144
  101.2 5.2 %collective-permute-start.7 = (bf16[48,3584]{1,0:T(8,128)(2,1)}, bf16[48,3584]{1,0:T(8,128)(2,1)}, u32[]{:S(2)}, u32[]{:S(2)}) collective-permute-start(bf16[48,3584]{1,0:T(8,128)(2,1)} %add_convert_fusion.11), channel_id=1, source_target_pairs={{0,2},{2,4},{4,6},{6,7},{7,5},{5,3},{3,1},{1,0},{8,10},{10,12},{12... | collective-permute-start | bytes 1032200 | tf_op jit(solution)/shard_map/ppermute | solution.py:147
  106.4 2.9 conditional.28
  109.3 6.3 %collective-permute-start.10 = (bf16[48,3584]{1,0:T(8,128)(2,1)}, bf16[48,3584]{1,0:T(8,128)(2,1)}, u32[]{:S(2)}, u32[]{:S(2)}) collective-permute-start(bf16[48,3584]{1,0:T(8,128)(2,1)} %collective-permute-done.8), channel_id=1, source_target_pairs={{0,2},{2,4},{4,6},{6,7},{7,5},{5,3},{3,1},{1,0},{8,10},{10,12},{12... | collective-permute-start | bytes 1032200 | tf_op jit(solution)/shard_map/ppermute | solution.py:144
  117.6 3.8 %collective-permute-start.9 = (bf16[48,3584]{1,0:T(8,128)(2,1)}, bf16[48,3584]{1,0:T(8,128)(2,1)}, u32[]{:S(2)}, u32[]{:S(2)}) collective-permute-start(bf16[48,3584]{1,0:T(8,128)(2,1)} %add_convert_fusion.10), channel_id=1, source_target_pairs={{0,2},{2,4},{4,6},{6,7},{7,5},{5,3},{3,1},{1,0},{8,10},{10,12},{12... | collective-permute-start | bytes 1032200 | tf_op jit(solution)/shard_map/ppermute | solution.py:147
  124.2 2.9 conditional.29
  127.0 6.5 %collective-permute-start.12 = (bf16[48,3584]{1,0:T(8,128)(2,1)}, bf16[48,3584]{1,0:T(8,128)(2,1)}, u32[]{:S(2)}, u32[]{:S(2)}) collective-permute-start(bf16[48,3584]{1,0:T(8,128)(2,1)} %collective-permute-done.10), channel_id=1, source_target_pairs={{0,2},{2,4},{4,6},{6,7},{7,5},{5,3},{3,1},{1,0},{8,10},{10,12},{12... | collective-permute-start | bytes 1032200 | tf_op jit(solution)/shard_map/ppermute | solution.py:144
  135.5 3.1 collective-permute-start.11
  140.9 2.9 conditional.30
  147.9 5.2 %collective-permute-start.13 = (bf16[48,3584]{1,0:T(8,128)(2,1)}, bf16[48,3584]{1,0:T(8,128)(2,1)}, u32[]{:S(2)}, u32[]{:S(2)}) collective-permute-start(bf16[48,3584]{1,0:T(8,128)(2,1)} %add_convert_fusion.8), channel_id=1, source_target_pairs={{0,2},{2,4},{4,6},{6,7},{7,5},{5,3},{3,1},{1,0},{8,10},{10,12},{12... | collective-permute-start | bytes 1032200 | tf_op jit(solution)/shard_map/ppermute | solution.py:147
  160.3 3.7 %all-to-all-start.1 = ((bf16[8,3,2,3584]{3,2,1,0:T(2,128)(2,1)}), bf16[8,3,2,3584]{3,2,1,0:T(2,128)(2,1)S(1)}, u32[]{:S(2)}, u32[]{:S(2)}) async-start(bf16[8,3,2,3584]{3,2,1,0:T(2,128)(2,1)} %reshape.50), calls=%async_computation.1 | async-start | bytes 688128 | tf_op jit(solution)/shard_map/all_to_all | solution.py:118
  164.7 11.9 %all-to-all-done.1 = bf16[8,3,2,3584]{3,2,1,0:T(2,128)(2,1)S(1)} async-done(((bf16[8,3,2,3584]{3,2,1,0:T(2,128)(2,1)}), bf16[8,3,2,3584]{3,2,1,0:T(2,128)(2,1)S(1)}, u32[]{:S(2)}, u32[]{:S(2)}) %all-to-all-start.1) | async-done | bytes 344096 | tf_op jit(solution)/shard_map/all_to_all | solution.py:118
  184.9 16.9 %all_to_all.20 = bf16[8,3,2,3584]{3,2,1,0:T(2,128)(2,1)} all-to-all(bf16[8,3,2,3584]{3,2,1,0:T(2,128)(2,1)S(1)} %reshape.52), channel_id=1, replica_groups={{0,15,16,31,32,47,48,63},{1,14,17,30,33,46,49,62},{2,13,18,29,34,45,50,..., dimensions={0} | all-to-all | bytes 688128 | tf_op jit(solution)/shard_map/all_to_all | solution.py:118
  202.9 10.9 %collective-permute-start.15 = (bf16[48,3584]{1,0:T(8,128)(2,1)S(1)}, bf16[48,3584]{1,0:T(8,128)(2,1)}, u32[]{:S(2)}, u32[]{:S(2)}) collective-permute-start(bf16[48,3584]{1,0:T(8,128)(2,1)S(1)} %reshape.53), channel_id=1, source_target_pairs={{0,2},{2,4},{4,6},{6,7},{7,5},{5,3},{3,1},{1,0},{8,10},{10,12},{12... | collective-permute-start | bytes 1032200 | tf_op jit(solution)/shard_map/ppermute | solution.py:144
  213.8 10.7 %collective-permute-done.15 = bf16[48,3584]{1,0:T(8,128)(2,1)} collective-permute-done((bf16[48,3584]{1,0:T(8,128)(2,1)S(1)}, bf16[48,3584]{1,0:T(8,128)(2,1)}, u32[]{:S(2)}, u32[]{:S(2)}) %collective-permute-start.15) | collective-permute-done | bytes 344096 | tf_op jit(solution)/shard_map/ppermute | solution.py:144
  226.8 3.7 conditional.32
  232.4 6.2 %collective-permute-done.17 = bf16[48,3584]{1,0:T(8,128)(2,1)} collective-permute-done((bf16[48,3584]{1,0:T(8,128)(2,1)}, bf16[48,3584]{1,0:T(8,128)(2,1)}, u32[]{:S(2)}, u32[]{:S(2)}) %collective-permute-start.17) | collective-permute-done | bytes 344096 | tf_op jit(solution)/shard_map/ppermute | solution.py:144
  238.6 3.8 %conditional.33 = (f32[48,3584]{1,0:T(8,128)}) conditional(s32[]{:T(128)} %convert_element_type.501, (bf16[48,3584]{1,0:T(8,128)(2,1)}, bf16[192,3584]{1,0:T(8,128)(2,1)}, bf16[48,384]{1,0:T(8,128)(2,1)}, bf16[3584,384]{1,0:T(8,128)(2,1)S(1)}) %tuple.276, (bf16[48,3584]{1,0:T(8,128)(2,1)}, bf16[3584,384]{1,0:T(8,128)(2,1)S(1)}, ...), branch_computations={%region_20.21_spmd, %region_21.22_spmd} | conditional | flops 198736896 | bytes 10838052 | solution.py:108
  242.3 3.5 collective-permute-start.19
  249.7 5.0 %collective-permute-done.19 = bf16[48,3584]{1,0:T(8,128)(2,1)} collective-permute-done((bf16[48,3584]{1,0:T(8,128)(2,1)}, bf16[48,3584]{1,0:T(8,128)(2,1)}, u32[]{:S(2)}, u32[]{:S(2)}) %collective-permute-start.19) | collective-permute-done | bytes 344096 | tf_op jit(solution)/shard_map/ppermute | solution.py:144
  254.8 3.8 %conditional.34 = (f32[48,3584]{1,0:T(8,128)}) conditional(s32[]{:T(128)} %convert_element_type.501, (bf16[48,3584]{1,0:T(8,128)(2,1)}, bf16[192,3584]{1,0:T(8,128)(2,1)}, bf16[48,384]{1,0:T(8,128)(2,1)}, bf16[3584,384]{1,0:T(8,128)(2,1)S(1)}) %tuple.278, (bf16[48,3584]{1,0:T(8,128)(2,1)}, bf16[3584,384]{1,0:T(8,128)(2,1)S(1)}, ...), branch_computations={%region_22.23_spmd, %region_23.24_spmd} | conditional | flops 198736896 | bytes 10838052 | solution.py:108
  258.5 4.8 %collective-permute-start.21 = (bf16[48,3584]{1,0:T(8,128)(2,1)}, bf16[48,3584]{1,0:T(8,128)(2,1)}, u32[]{:S(2)}, u32[]{:S(2)}) collective-permute-start(bf16[48,3584]{1,0:T(8,128)(2,1)} %collective-permute-done.19), channel_id=1, source_target_pairs={{0,2},{2,4},{4,6},{6,7},{7,5},{5,3},{3,1},{1,0},{8,10},{10,12},{12... | collective-permute-start | bytes 1032200 | tf_op jit(solution)/shard_map/ppermute | solution.py:144
  265.3 3.6 collective-permute-start.20
  268.9 3.1 collective-permute-done.21
  272.0 3.8 %conditional.35 = (f32[48,3584]{1,0:T(8,128)}) conditional(s32[]{:T(128)} %convert_element_type.501, (bf16[48,3584]{1,0:T(8,128)(2,1)}, bf16[192,3584]{1,0:T(8,128)(2,1)}, bf16[48,384]{1,0:T(8,128)(2,1)}, bf16[3584,384]{1,0:T(8,128)(2,1)S(1)}) %tuple.280, (bf16[48,3584]{1,0:T(8,128)(2,1)}, bf16[3584,384]{1,0:T(8,128)(2,1)S(1)}, ...), branch_computations={%region_24.25_spmd, %region_25.26_spmd} | conditional | flops 198736896 | bytes 10838052 | solution.py:108
  275.8 6.3 %collective-permute-start.23 = (bf16[48,3584]{1,0:T(8,128)(2,1)}, bf16[48,3584]{1,0:T(8,128)(2,1)}, u32[]{:S(2)}, u32[]{:S(2)}) collective-permute-start(bf16[48,3584]{1,0:T(8,128)(2,1)} %collective-permute-done.21), channel_id=1, source_target_pairs={{0,2},{2,4},{4,6},{6,7},{7,5},{5,3},{3,1},{1,0},{8,10},{10,12},{12... | collective-permute-start | bytes 1032200 | tf_op jit(solution)/shard_map/ppermute | solution.py:144
  284.1 3.6 collective-permute-start.22
  288.7 3.8 %conditional.36 = (f32[48,3584]{1,0:T(8,128)}) conditional(s32[]{:T(128)} %convert_element_type.501, (bf16[48,3584]{1,0:T(8,128)(2,1)}, bf16[192,3584]{1,0:T(8,128)(2,1)}, bf16[48,384]{1,0:T(8,128)(2,1)S(1)}, bf16[3584,384]{1,0:T(8,128)(2,1)S(1)}) %tuple.282, (bf16[48,3584]{1,0:T(8,128)(2,1)}, bf16[3584,384]{1,0:T(8,128)(2,1)S(1)}, ...), branch_computations={%region_26.27_spmd, %region_27.28_spmd} | conditional | flops 198736896 | bytes 10838052 | solution.py:108
  292.5 6.5 %collective-permute-start.25 = (bf16[48,3584]{1,0:T(8,128)(2,1)}, bf16[48,3584]{1,0:T(8,128)(2,1)}, u32[]{:S(2)}, u32[]{:S(2)}) collective-permute-start(bf16[48,3584]{1,0:T(8,128)(2,1)} %collective-permute-done.23), channel_id=1, source_target_pairs={{0,2},{2,4},{4,6},{6,7},{7,5},{5,3},{3,1},{1,0},{8,10},{10,12},{12... | collective-permute-start | bytes 1032200 | tf_op jit(solution)/shard_map/ppermute | solution.py:144
  301.0 3.8 %collective-permute-start.24 = (bf16[48,3584]{1,0:T(8,128)(2,1)}, bf16[48,3584]{1,0:T(8,128)(2,1)}, u32[]{:S(2)}, u32[]{:S(2)}) collective-permute-start(bf16[48,3584]{1,0:T(8,128)(2,1)} %add_convert_fusion.3), channel_id=1, source_target_pairs={{0,2},{2,4},{4,6},{6,7},{7,5},{5,3},{3,1},{1,0},{8,10},{10,12},{12... | collective-permute-start | bytes 1032200 | tf_op jit(solution)/shard_map/ppermute | solution.py:147
  304.8 3.8 %conditional.37 = (f32[48,3584]{1,0:T(8,128)}) conditional(s32[]{:T(128)} %convert_element_type.501, (bf16[48,3584]{1,0:T(8,128)(2,1)}, bf16[192,3584]{1,0:T(8,128)(2,1)}, bf16[48,384]{1,0:T(8,128)(2,1)S(1)}, bf16[3584,384]{1,0:T(8,128)(2,1)S(1)}) %tuple.284, (bf16[48,3584]{1,0:T(8,128)(2,1)}, bf16[3584,384]{1,0:T(8,128)(2,1)S(1)}, ...), branch_computations={%region_28.29_spmd, %region_29.30_spmd} | conditional | flops 198736896 | bytes 10838052 | solution.py:108
  308.7 5.7 %collective-permute-start.27 = (bf16[48,3584]{1,0:T(8,128)(2,1)}, bf16[48,3584]{1,0:T(8,128)(2,1)}, u32[]{:S(2)}, u32[]{:S(2)}) collective-permute-start(bf16[48,3584]{1,0:T(8,128)(2,1)} %collective-permute-done.25), channel_id=1, source_target_pairs={{0,2},{2,4},{4,6},{6,7},{7,5},{5,3},{3,1},{1,0},{8,10},{10,12},{12... | collective-permute-start | bytes 1032200 | tf_op jit(solution)/shard_map/ppermute | solution.py:144
  316.4 5.6 %collective-permute-start.26 = (bf16[48,3584]{1,0:T(8,128)(2,1)}, bf16[48,3584]{1,0:T(8,128)(2,1)}, u32[]{:S(2)}, u32[]{:S(2)}) collective-permute-start(bf16[48,3584]{1,0:T(8,128)(2,1)} %add_convert_fusion.2), channel_id=1, source_target_pairs={{0,2},{2,4},{4,6},{6,7},{7,5},{5,3},{3,1},{1,0},{8,10},{10,12},{12... | collective-permute-start | bytes 1032200 | tf_op jit(solution)/shard_map/ppermute | solution.py:147
  322.0 4.1 %conditional.38 = (f32[48,3584]{1,0:T(8,128)}) conditional(s32[]{:T(128)} %convert_element_type.501, (bf16[48,3584]{1,0:T(8,128)(2,1)}, bf16[192,3584]{1,0:T(8,128)(2,1)}, bf16[48,384]{1,0:T(8,128)(2,1)S(1)}, bf16[3584,384]{1,0:T(8,128)(2,1)S(1)}) %tuple.286, (bf16[48,3584]{1,0:T(8,128)(2,1)}, bf16[3584,384]{1,0:T(8,128)(2,1)S(1)}, ...), branch_computations={%region_30.31_spmd, %region_31.32_spmd} | conditional | flops 198736896 | bytes 10838052 | solution.py:108
  329.0 6.5 %collective-permute-start.28 = (bf16[48,3584]{1,0:T(8,128)(2,1)}, bf16[48,3584]{1,0:T(8,128)(2,1)}, u32[]{:S(2)}, u32[]{:S(2)}) collective-permute-start(bf16[48,3584]{1,0:T(8,128)(2,1)} %add_convert_fusion.1), channel_id=1, source_target_pairs={{0,2},{2,4},{4,6},{6,7},{7,5},{5,3},{3,1},{1,0},{8,10},{10,12},{12... | collective-permute-start | bytes 1032200 | tf_op jit(solution)/shard_map/ppermute | solution.py:147
  335.5 3.7 %conditional.39 = (f32[48,3584]{1,0:T(8,128)}) conditional(s32[]{:T(128)} %convert_element_type.501, (bf16[48,3584]{1,0:T(8,128)(2,1)S(1)}, bf16[192,3584]{1,0:T(8,128)(2,1)}, bf16[48,384]{1,0:T(8,128)(2,1)S(1)}, bf16[3584,384]{1,0:T(8,128)(2,1)S(1)}) %tuple.288, (bf16[48,3584]{1,0:T(8,128)(2,1)S(1)}, bf16[3584,384]{1,0:T(8,128)(2,1)S(1)}, ...), branch_computations={%region_32.33_spmd, %region_33.34_spmd} | conditional | flops 198736896 | bytes 10838052 | solution.py:108
  342.6 23.4 %all_to_all.21 = bf16[8,3,2,3584]{3,2,1,0:T(2,128)(2,1)S(1)} all-to-all(bf16[8,3,2,3584]{3,2,1,0:T(2,128)(2,1)S(1)} %reshape.54), channel_id=1, replica_groups={{0,15,16,31,32,47,48,63},{1,14,17,30,33,46,49,62},{2,13,18,29,34,45,50,..., dimensions={0} | all-to-all | bytes 688128 | tf_op jit(solution)/shard_map/all_to_all | solution.py:118
  (128 shorter events, 133.3 us)
Async XLA Ops:
  0.0 38.8 %copy-start = (bf16[1,1,384,384]{3,2,1,0:T(8,128)(2,1)S(1)}, bf16[1,1,384,384]{3,2,1,0:T(8,128)(2,1)}, u32[]{:S(2)}) copy-start(bf16[1,1,384,384]{3,2,1,0:T(8,128)(2,1)} %param.40) | copy-start | bytes 884740
  0.0 51.3 %copy-start.1 = (bf16[1,1,3584,384]{3,2,1,0:T(8,128)(2,1)S(1)}, bf16[1,1,3584,384]{3,2,1,0:T(8,128)(2,1)}, u32[]{:S(2)}) copy-start(bf16[1,1,3584,384]{3,2,1,0:T(8,128)(2,1)} %param.43) | copy-start | bytes 8257540
  3.7 30.3 %all-to-all-start = ((bf16[8,3,2,3584]{3,2,1,0:T(2,128)(2,1)}), bf16[8,3,2,3584]{3,2,1,0:T(2,128)(2,1)}, u32[]{:S(2)}, u32[]{:S(2)}) async-start(bf16[8,3,2,3584]{3,2,1,0:T(2,128)(2,1)} %reshape.48), calls=%async_computation | async-start | bytes 688128 | tf_op jit(solution)/shard_map/all_to_all | solution.py:118
  35.1 11.5 %collective-permute-start = (bf16[48,3584]{1,0:T(8,128)(2,1)S(1)}, bf16[48,3584]{1,0:T(8,128)(2,1)}, u32[]{:S(2)}, u32[]{:S(2)}) collective-permute-start(bf16[48,3584]{1,0:T(8,128)(2,1)S(1)} %reshape.49), channel_id=1, source_target_pairs={{0,2},{2,4},{4,6},{6,7},{7,5},{5,3},{3,1},{1,0},{8,10},{10,12},{12... | collective-permute-start | bytes 1032200 | tf_op jit(solution)/shard_map/ppermute | solution.py:144
  41.4 9.8 %copy-start.22 = (bf16[48,384]{1,0:T(8,128)(2,1)}, bf16[48,384]{1,0:T(8,128)(2,1)S(1)}, u32[]{:S(2)}) copy-start(bf16[48,384]{1,0:T(8,128)(2,1)S(1)} %get-tuple-element.439) | copy-start | bytes 110596
  46.6 11.7 %collective-permute-start.2 = (bf16[48,3584]{1,0:T(8,128)(2,1)}, bf16[48,3584]{1,0:T(8,128)(2,1)}, u32[]{:S(2)}, u32[]{:S(2)}) collective-permute-start(bf16[48,3584]{1,0:T(8,128)(2,1)} %collective-permute-done), channel_id=1, source_target_pairs={{0,2},{2,4},{4,6},{6,7},{7,5},{5,3},{3,1},{1,0},{8,10},{10,12},{12... | collective-permute-start | bytes 1032200 | tf_op jit(solution)/shard_map/ppermute | solution.py:144
  51.3 1.6 copy-start.2
  54.1 13.6 %collective-permute-start.1 = (bf16[48,3584]{1,0:T(8,128)(2,1)}, bf16[48,3584]{1,0:T(8,128)(2,1)}, u32[]{:S(2)}, u32[]{:S(2)}) collective-permute-start(bf16[48,3584]{1,0:T(8,128)(2,1)} %get-tuple-element.455), channel_id=1, source_target_pairs={{0,2},{2,4},{4,6},{6,7},{7,5},{5,3},{3,1},{1,0},{8,10},{10,12},{12... | collective-permute-start | bytes 1032200 | tf_op jit(solution)/shard_map/ppermute | solution.py:147
  58.4 1.6 copy-start.3
  61.2 13.2 %collective-permute-start.4 = (bf16[48,3584]{1,0:T(8,128)(2,1)}, bf16[48,3584]{1,0:T(8,128)(2,1)}, u32[]{:S(2)}, u32[]{:S(2)}) collective-permute-start(bf16[48,3584]{1,0:T(8,128)(2,1)} %collective-permute-done.2), channel_id=1, source_target_pairs={{0,2},{2,4},{4,6},{6,7},{7,5},{5,3},{3,1},{1,0},{8,10},{10,12},{12... | collective-permute-start | bytes 1032200 | tf_op jit(solution)/shard_map/ppermute | solution.py:144
  69.7 14.0 %collective-permute-start.3 = (bf16[48,3584]{1,0:T(8,128)(2,1)}, bf16[48,3584]{1,0:T(8,128)(2,1)}, u32[]{:S(2)}, u32[]{:S(2)}) collective-permute-start(bf16[48,3584]{1,0:T(8,128)(2,1)} %add_convert_fusion.13), channel_id=1, source_target_pairs={{0,2},{2,4},{4,6},{6,7},{7,5},{5,3},{3,1},{1,0},{8,10},{10,12},{12... | collective-permute-start | bytes 1032200 | tf_op jit(solution)/shard_map/ppermute | solution.py:147
  74.5 1.6 copy-start.4
  77.4 12.8 %collective-permute-start.6 = (bf16[48,3584]{1,0:T(8,128)(2,1)}, bf16[48,3584]{1,0:T(8,128)(2,1)}, u32[]{:S(2)}, u32[]{:S(2)}) collective-permute-start(bf16[48,3584]{1,0:T(8,128)(2,1)} %collective-permute-done.4), channel_id=1, source_target_pairs={{0,2},{2,4},{4,6},{6,7},{7,5},{5,3},{3,1},{1,0},{8,10},{10,12},{12... | collective-permute-start | bytes 1032200 | tf_op jit(solution)/shard_map/ppermute | solution.py:144
  85.7 13.6 %collective-permute-start.5 = (bf16[48,3584]{1,0:T(8,128)(2,1)}, bf16[48,3584]{1,0:T(8,128)(2,1)}, u32[]{:S(2)}, u32[]{:S(2)}) collective-permute-start(bf16[48,3584]{1,0:T(8,128)(2,1)} %add_convert_fusion.12), channel_id=1, source_target_pairs={{0,2},{2,4},{4,6},{6,7},{7,5},{5,3},{3,1},{1,0},{8,10},{10,12},{12... | collective-permute-start | bytes 1032200 | tf_op jit(solution)/shard_map/ppermute | solution.py:147
  90.2 1.6 copy-start.5
  93.1 13.3 %collective-permute-start.8 = (bf16[48,3584]{1,0:T(8,128)(2,1)}, bf16[48,3584]{1,0:T(8,128)(2,1)}, u32[]{:S(2)}, u32[]{:S(2)}) collective-permute-start(bf16[48,3584]{1,0:T(8,128)(2,1)} %collective-permute-done.6), channel_id=1, source_target_pairs={{0,2},{2,4},{4,6},{6,7},{7,5},{5,3},{3,1},{1,0},{8,10},{10,12},{12... | collective-permute-start | bytes 1032200 | tf_op jit(solution)/shard_map/ppermute | solution.py:144
  101.2 14.4 %collective-permute-start.7 = (bf16[48,3584]{1,0:T(8,128)(2,1)}, bf16[48,3584]{1,0:T(8,128)(2,1)}, u32[]{:S(2)}, u32[]{:S(2)}) collective-permute-start(bf16[48,3584]{1,0:T(8,128)(2,1)} %add_convert_fusion.11), channel_id=1, source_target_pairs={{0,2},{2,4},{4,6},{6,7},{7,5},{5,3},{3,1},{1,0},{8,10},{10,12},{12... | collective-permute-start | bytes 1032200 | tf_op jit(solution)/shard_map/ppermute | solution.py:147
  106.4 1.6 copy-start.6
  109.3 14.9 %collective-permute-start.10 = (bf16[48,3584]{1,0:T(8,128)(2,1)}, bf16[48,3584]{1,0:T(8,128)(2,1)}, u32[]{:S(2)}, u32[]{:S(2)}) collective-permute-start(bf16[48,3584]{1,0:T(8,128)(2,1)} %collective-permute-done.8), channel_id=1, source_target_pairs={{0,2},{2,4},{4,6},{6,7},{7,5},{5,3},{3,1},{1,0},{8,10},{10,12},{12... | collective-permute-start | bytes 1032200 | tf_op jit(solution)/shard_map/ppermute | solution.py:144
  117.6 15.9 %collective-permute-start.9 = (bf16[48,3584]{1,0:T(8,128)(2,1)}, bf16[48,3584]{1,0:T(8,128)(2,1)}, u32[]{:S(2)}, u32[]{:S(2)}) collective-permute-start(bf16[48,3584]{1,0:T(8,128)(2,1)} %add_convert_fusion.10), channel_id=1, source_target_pairs={{0,2},{2,4},{4,6},{6,7},{7,5},{5,3},{3,1},{1,0},{8,10},{10,12},{12... | collective-permute-start | bytes 1032200 | tf_op jit(solution)/shard_map/ppermute | solution.py:147
  124.2 1.6 copy-start.7
  127.0 13.9 %collective-permute-start.12 = (bf16[48,3584]{1,0:T(8,128)(2,1)}, bf16[48,3584]{1,0:T(8,128)(2,1)}, u32[]{:S(2)}, u32[]{:S(2)}) collective-permute-start(bf16[48,3584]{1,0:T(8,128)(2,1)} %collective-permute-done.10), channel_id=1, source_target_pairs={{0,2},{2,4},{4,6},{6,7},{7,5},{5,3},{3,1},{1,0},{8,10},{10,12},{12... | collective-permute-start | bytes 1032200 | tf_op jit(solution)/shard_map/ppermute | solution.py:144
  135.5 10.3 %collective-permute-start.11 = (bf16[48,3584]{1,0:T(8,128)(2,1)}, bf16[48,3584]{1,0:T(8,128)(2,1)}, u32[]{:S(2)}, u32[]{:S(2)}) collective-permute-start(bf16[48,3584]{1,0:T(8,128)(2,1)} %add_convert_fusion.9), channel_id=1, source_target_pairs={{0,2},{2,4},{4,6},{6,7},{7,5},{5,3},{3,1},{1,0},{8,10},{10,12},{12... | collective-permute-start | bytes 1032200 | tf_op jit(solution)/shard_map/ppermute | solution.py:147
  140.9 1.6 copy-start.8
  147.9 10.3 %collective-permute-start.13 = (bf16[48,3584]{1,0:T(8,128)(2,1)}, bf16[48,3584]{1,0:T(8,128)(2,1)}, u32[]{:S(2)}, u32[]{:S(2)}) collective-permute-start(bf16[48,3584]{1,0:T(8,128)(2,1)} %add_convert_fusion.8), channel_id=1, source_target_pairs={{0,2},{2,4},{4,6},{6,7},{7,5},{5,3},{3,1},{1,0},{8,10},{10,12},{12... | collective-permute-start | bytes 1032200 | tf_op jit(solution)/shard_map/ppermute | solution.py:147
  153.3 1.3 copy-start.9
  160.3 16.3 %all-to-all-start.1 = ((bf16[8,3,2,3584]{3,2,1,0:T(2,128)(2,1)}), bf16[8,3,2,3584]{3,2,1,0:T(2,128)(2,1)S(1)}, u32[]{:S(2)}, u32[]{:S(2)}) async-start(bf16[8,3,2,3584]{3,2,1,0:T(2,128)(2,1)} %reshape.50), calls=%async_computation.1 | async-start | bytes 688128 | tf_op jit(solution)/shard_map/all_to_all | solution.py:118
  178.7 3.4 copy-start.18
  178.8 3.4 collective-permute-start.14
  182.1 0.7 copy-start.20
  202.9 21.6 %collective-permute-start.15 = (bf16[48,3584]{1,0:T(8,128)(2,1)S(1)}, bf16[48,3584]{1,0:T(8,128)(2,1)}, u32[]{:S(2)}, u32[]{:S(2)}) collective-permute-start(bf16[48,3584]{1,0:T(8,128)(2,1)S(1)} %reshape.53), channel_id=1, source_target_pairs={{0,2},{2,4},{4,6},{6,7},{7,5},{5,3},{3,1},{1,0},{8,10},{10,12},{12... | collective-permute-start | bytes 1032200 | tf_op jit(solution)/shard_map/ppermute | solution.py:144
  224.5 14.0 %collective-permute-start.17 = (bf16[48,3584]{1,0:T(8,128)(2,1)}, bf16[48,3584]{1,0:T(8,128)(2,1)}, u32[]{:S(2)}, u32[]{:S(2)}) collective-permute-start(bf16[48,3584]{1,0:T(8,128)(2,1)} %collective-permute-done.15), channel_id=1, source_target_pairs={{0,2},{2,4},{4,6},{6,7},{7,5},{5,3},{3,1},{1,0},{8,10},{10,12},{12... | collective-permute-start | bytes 1032200 | tf_op jit(solution)/shard_map/ppermute | solution.py:144
  230.4 15.3 %collective-permute-start.16 = (bf16[48,3584]{1,0:T(8,128)(2,1)}, bf16[48,3584]{1,0:T(8,128)(2,1)}, u32[]{:S(2)}, u32[]{:S(2)}) collective-permute-start(bf16[48,3584]{1,0:T(8,128)(2,1)} %get-tuple-element.463), channel_id=1, source_target_pairs={{0,2},{2,4},{4,6},{6,7},{7,5},{5,3},{3,1},{1,0},{8,10},{10,12},{12... | collective-permute-start | bytes 1032200 | tf_op jit(solution)/shard_map/ppermute | solution.py:147
  242.3 12.4 %collective-permute-start.19 = (bf16[48,3584]{1,0:T(8,128)(2,1)}, bf16[48,3584]{1,0:T(8,128)(2,1)}, u32[]{:S(2)}, u32[]{:S(2)}) collective-permute-start(bf16[48,3584]{1,0:T(8,128)(2,1)} %collective-permute-done.17), channel_id=1, source_target_pairs={{0,2},{2,4},{4,6},{6,7},{7,5},{5,3},{3,1},{1,0},{8,10},{10,12},{12... | collective-permute-start | bytes 1032200 | tf_op jit(solution)/shard_map/ppermute | solution.py:144
  247.8 15.6 %collective-permute-start.18 = (bf16[48,3584]{1,0:T(8,128)(2,1)}, bf16[48,3584]{1,0:T(8,128)(2,1)}, u32[]{:S(2)}, u32[]{:S(2)}) collective-permute-start(bf16[48,3584]{1,0:T(8,128)(2,1)} %add_convert_fusion.6), channel_id=1, source_target_pairs={{0,2},{2,4},{4,6},{6,7},{7,5},{5,3},{3,1},{1,0},{8,10},{10,12},{12... | collective-permute-start | bytes 1032200 | tf_op jit(solution)/shard_map/ppermute | solution.py:147
  258.5 13.5 %collective-permute-start.21 = (bf16[48,3584]{1,0:T(8,128)(2,1)}, bf16[48,3584]{1,0:T(8,128)(2,1)}, u32[]{:S(2)}, u32[]{:S(2)}) collective-permute-start(bf16[48,3584]{1,0:T(8,128)(2,1)} %collective-permute-done.19), channel_id=1, source_target_pairs={{0,2},{2,4},{4,6},{6,7},{7,5},{5,3},{3,1},{1,0},{8,10},{10,12},{12... | collective-permute-start | bytes 1032200 | tf_op jit(solution)/shard_map/ppermute | solution.py:144
  265.3 16.8 %collective-permute-start.20 = (bf16[48,3584]{1,0:T(8,128)(2,1)}, bf16[48,3584]{1,0:T(8,128)(2,1)}, u32[]{:S(2)}, u32[]{:S(2)}) collective-permute-start(bf16[48,3584]{1,0:T(8,128)(2,1)} %add_convert_fusion.5), channel_id=1, source_target_pairs={{0,2},{2,4},{4,6},{6,7},{7,5},{5,3},{3,1},{1,0},{8,10},{10,12},{12... | collective-permute-start | bytes 1032200 | tf_op jit(solution)/shard_map/ppermute | solution.py:147
  275.8 12.9 %collective-permute-start.23 = (bf16[48,3584]{1,0:T(8,128)(2,1)}, bf16[48,3584]{1,0:T(8,128)(2,1)}, u32[]{:S(2)}, u32[]{:S(2)}) collective-permute-start(bf16[48,3584]{1,0:T(8,128)(2,1)} %collective-permute-done.21), channel_id=1, source_target_pairs={{0,2},{2,4},{4,6},{6,7},{7,5},{5,3},{3,1},{1,0},{8,10},{10,12},{12... | collective-permute-start | bytes 1032200 | tf_op jit(solution)/shard_map/ppermute | solution.py:144
  284.1 15.0 %collective-permute-start.22 = (bf16[48,3584]{1,0:T(8,128)(2,1)}, bf16[48,3584]{1,0:T(8,128)(2,1)}, u32[]{:S(2)}, u32[]{:S(2)}) collective-permute-start(bf16[48,3584]{1,0:T(8,128)(2,1)} %add_convert_fusion.4), channel_id=1, source_target_pairs={{0,2},{2,4},{4,6},{6,7},{7,5},{5,3},{3,1},{1,0},{8,10},{10,12},{12... | collective-permute-start | bytes 1032200 | tf_op jit(solution)/shard_map/ppermute | solution.py:147
  292.5 12.3 %collective-permute-start.25 = (bf16[48,3584]{1,0:T(8,128)(2,1)}, bf16[48,3584]{1,0:T(8,128)(2,1)}, u32[]{:S(2)}, u32[]{:S(2)}) collective-permute-start(bf16[48,3584]{1,0:T(8,128)(2,1)} %collective-permute-done.23), channel_id=1, source_target_pairs={{0,2},{2,4},{4,6},{6,7},{7,5},{5,3},{3,1},{1,0},{8,10},{10,12},{12... | collective-permute-start | bytes 1032200 | tf_op jit(solution)/shard_map/ppermute | solution.py:144
  301.0 13.4 %collective-permute-start.24 = (bf16[48,3584]{1,0:T(8,128)(2,1)}, bf16[48,3584]{1,0:T(8,128)(2,1)}, u32[]{:S(2)}, u32[]{:S(2)}) collective-permute-start(bf16[48,3584]{1,0:T(8,128)(2,1)} %add_convert_fusion.3), channel_id=1, source_target_pairs={{0,2},{2,4},{4,6},{6,7},{7,5},{5,3},{3,1},{1,0},{8,10},{10,12},{12... | collective-permute-start | bytes 1032200 | tf_op jit(solution)/shard_map/ppermute | solution.py:147
  308.7 13.3 %collective-permute-start.27 = (bf16[48,3584]{1,0:T(8,128)(2,1)}, bf16[48,3584]{1,0:T(8,128)(2,1)}, u32[]{:S(2)}, u32[]{:S(2)}) collective-permute-start(bf16[48,3584]{1,0:T(8,128)(2,1)} %collective-permute-done.25), channel_id=1, source_target_pairs={{0,2},{2,4},{4,6},{6,7},{7,5},{5,3},{3,1},{1,0},{8,10},{10,12},{12... | collective-permute-start | bytes 1032200 | tf_op jit(solution)/shard_map/ppermute | solution.py:144
  316.4 10.7 %collective-permute-start.26 = (bf16[48,3584]{1,0:T(8,128)(2,1)}, bf16[48,3584]{1,0:T(8,128)(2,1)}, u32[]{:S(2)}, u32[]{:S(2)}) collective-permute-start(bf16[48,3584]{1,0:T(8,128)(2,1)} %add_convert_fusion.2), channel_id=1, source_target_pairs={{0,2},{2,4},{4,6},{6,7},{7,5},{5,3},{3,1},{1,0},{8,10},{10,12},{12... | collective-permute-start | bytes 1032200 | tf_op jit(solution)/shard_map/ppermute | solution.py:147
  329.0 12.2 %collective-permute-start.28 = (bf16[48,3584]{1,0:T(8,128)(2,1)}, bf16[48,3584]{1,0:T(8,128)(2,1)}, u32[]{:S(2)}, u32[]{:S(2)}) collective-permute-start(bf16[48,3584]{1,0:T(8,128)(2,1)} %add_convert_fusion.1), channel_id=1, source_target_pairs={{0,2},{2,4},{4,6},{6,7},{7,5},{5,3},{3,1},{1,0},{8,10},{10,12},{12... | collective-permute-start | bytes 1032200 | tf_op jit(solution)/shard_map/ppermute | solution.py:147
  339.2 26.9 %copy-start.21 = (bf16[32,3584]{1,0:T(8,128)(2,1)S(1)}, bf16[32,3584]{1,0:T(8,128)(2,1)}, u32[]{:S(2)}) copy-start(bf16[32,3584]{1,0:T(8,128)(2,1)} %copy-done.20) | copy-start | bytes 688132
  339.2 27.2 %copy-start.19 = (bf16[32,3584]{1,0:T(8,128)(2,1)S(1)}, bf16[32,3584]{1,0:T(8,128)(2,1)}, u32[]{:S(2)}) copy-start(bf16[32,3584]{1,0:T(8,128)(2,1)} %copy-done.18) | copy-start | bytes 688132

commit v4 on v3

--- a/solution.py
+++ b/solution.py
@@ -31,16 +31,15 @@
     return (slot_range[:, None] == targets[None, :]).astype(jnp.bfloat16)
 
 
-def expert_forward(token_rows, w_in_dev, w_out_dev):
+def forward_hidden(token_rows, w_in_dev, half_width):
     pre_act = jnp.dot(token_rows, w_in_dev, preferred_element_type=jnp.float32)
-    half_width = w_out_dev.shape[0]
     gate_vals = pre_act[:, :half_width]
     up_vals = pre_act[:, half_width:]
     hidden = (jax.nn.silu(gate_vals) * up_vals).astype(jnp.bfloat16)
-    return jnp.dot(hidden, w_out_dev, preferred_element_type=jnp.float32).astype(jnp.bfloat16)
+    return jnp.concatenate([hidden, jnp.zeros_like(hidden)], axis=1)
 
 
-def expert_backward(grad_rows, saved_pre, w_in_dev, w_out_dev):
+def backward_hidden(grad_rows, saved_pre, w_out_dev):
     half_width = w_out_dev.shape[0]
     gate_vals = saved_pre[:, :half_width].astype(jnp.float32)
     up_vals = saved_pre[:, half_width:].astype(jnp.float32)
@@ -49,10 +48,26 @@
     )
     d_gate = d_hidden * up_vals * silu_slope(gate_vals)
     d_up = d_hidden * jax.nn.silu(gate_vals)
-    d_pre = jnp.concatenate([d_gate, d_up], axis=1).astype(jnp.bfloat16)
-    return lax.dot_general(
+    return jnp.concatenate([d_gate, d_up], axis=1).astype(jnp.bfloat16)
+
+
+def joined(part, total):
+    if total is not None:
+        part = part + total.astype(jnp.float32)
+    return part.astype(jnp.bfloat16)
+
+
+def forward_out(hidden, total, w_out_dev):
+    half_width = w_out_dev.shape[0]
+    part = jnp.dot(hidden[:, :half_width], w_out_dev, preferred_element_type=jnp.float32)
+    return lax.optimization_barrier(joined(part, total))
+
+
+def backward_out(d_pre, total, w_in_dev):
+    part = lax.dot_general(
         d_pre, w_in_dev, (((1,), (1,)), ((), ())), preferred_element_type=jnp.float32
-    ).astype(jnp.bfloat16)
+    )
+    return lax.optimization_barrier(joined(part, total))
 
 
 def ring_of(first, size):
@@ -104,15 +119,19 @@
     current = entering[0]
     collected = []
 
-    def run_expert(rows, saved_rows, doing_forward):
+    def start_expert(rows, saved_rows, doing_forward):
         return lax.cond(
             doing_forward,
-            lambda: expert_forward(rows, w_in_dev, w_out_dev),
-            lambda: expert_backward(rows, saved_rows, w_in_dev, w_out_dev),
+            lambda: forward_hidden(rows, w_in_dev, w_out_dev.shape[0]),
+            lambda: backward_hidden(rows, saved_rows, w_out_dev),
         )
 
-    def added(left, right):
-        return (left.astype(jnp.float32) + right.astype(jnp.float32)).astype(jnp.bfloat16)
+    def end_expert(hidden, total, doing_forward):
+        return lax.cond(
+            doing_forward,
+            lambda: forward_out(hidden, total, w_out_dev),
+            lambda: backward_out(hidden, total, w_in_dev),
+        )
 
     def meet(rows):
         return lax.all_to_all(
@@ -138,14 +157,14 @@
             jnp.bfloat16
         )
         block = meet(token_rows)
-        own = run_expert(block, saved_blocks[0], doing_forward)
+        own = start_expert(block, saved_blocks[0], doing_forward)
         total = None
         for step in range(1, QUAD):
             block = lax.ppermute(block, "expert", ring_pairs)
-            result = run_expert(block, saved_blocks[step], doing_forward)
-            total = result if total is None else added(total, result)
+            hidden = start_expert(block, saved_blocks[step], doing_forward)
+            total = end_expert(hidden, total, doing_forward)
             total = lax.ppermute(total, "expert", ring_pairs)
-        total = added(total, own)
+        total = end_expert(own, total, doing_forward)
         picked = lax.dot_general(
             placed, meet(total), (((0,), (0,)), ((), ())), preferred_element_type=jnp.float32
         )

time: 369 us -> 359 us (0.973)
  the two profiles are of different devices: /device:TPU:70 before, /device:TPU:102 now
where the time goes in v4:
time: 359 us; the launch traced here: 357 us
  waiting for transfers between devices  140 us (39%)
  starting transfers between devices  94.4 us (26%)
  matrix products  71.1 us (20%)
  blocking collectives  37.2 us (10%)
  local copies, waits for them, and re-layouts  10.1 us (3%)
    ppermute x14, waiting for transfers between devices, shards(): total = lax.ppermute(total, 'expert', ring_pairs)  71.8 us
    ppermute x14, starting transfers between devices, shards(): block = lax.ppermute(block, 'expert', ring_pairs)  42.3 us
    ppermute x14, waiting for transfers between devices, shards(): block = lax.ppermute(block, 'expert', ring_pairs)  38.3 us
    all_to_all x2, blocking collectives, meet(): lax.all_to_all(rows.reshape(quads, capacity // 2, 2, row_width), 'expert'...  37.2 us
    ppermute x14, starting transfers between devices, shards(): total = lax.ppermute(total, 'expert', ring_pairs)  32.1 us
    all_to_all x2, waiting for transfers between devices, meet(): lax.all_to_all(rows.reshape(quads, capacity // 2, 2, row_width), 'expert'...  28.7 us
    dot_general x8, matrix products, backward_out(): lax.dot_general(d_pre, w_in_dev, (((1,), (1,)), ((), ())), preferred_elem...  19.7 us
    dot_general x8, matrix products, forward_out(): jnp.dot(hidden[:, :half_width], w_out_dev, preferred_element_type=jnp.flo...  19 us
  transfers between devices with their start and end apart: 31, of which 28 were waited for; matrix products, arithmetic and copies ran while one was open for 17% of the time, Pallas kernels for 0%

profile of v4, /device:TPU:102, one launch (start us, length us, event | category | flops | bytes accessed | tf_op | source)
XLA Modules:
  0.0 356.7 jit_solution(8640657201674453217)
XLA Ops:
  3.7 13.4 %all-to-all-start = ((bf16[8,3,2,3584]{3,2,1,0:T(2,128)(2,1)}), bf16[8,3,2,3584]{3,2,1,0:T(2,128)(2,1)}, u32[]{:S(2)}, u32[]{:S(2)}) async-start(bf16[8,3,2,3584]{3,2,1,0:T(2,128)(2,1)} %reshape.48), calls=%async_computation | async-start | bytes 688128 | tf_op jit(solution)/shard_map/all_to_all | solution.py:137
  17.8 14.3 %all-to-all-done = bf16[8,3,2,3584]{3,2,1,0:T(2,128)(2,1)} async-done(((bf16[8,3,2,3584]{3,2,1,0:T(2,128)(2,1)}), bf16[8,3,2,3584]{3,2,1,0:T(2,128)(2,1)}, u32[]{:S(2)}, u32[]{:S(2)}) %all-to-all-start) | async-done | bytes 344096 | tf_op jit(solution)/shard_map/all_to_all | solution.py:137
  33.3 5.2 %collective-permute-start = (bf16[48,3584]{1,0:T(8,128)(2,1)S(1)}, bf16[48,3584]{1,0:T(8,128)(2,1)}, u32[]{:S(2)}, u32[]{:S(2)}) collective-permute-start(bf16[48,3584]{1,0:T(8,128)(2,1)S(1)} %reshape.49), channel_id=1, source_target_pairs={{0,2},{2,4},{4,6},{6,7},{7,5},{5,3},{3,1},{1,0},{8,10},{10,12},{12... | collective-permute-start | bytes 1032200 | tf_op jit(solution)/shard_map/ppermute | solution.py:163
  41.2 4.6 %collective-permute-done = bf16[48,3584]{1,0:T(8,128)(2,1)} collective-permute-done((bf16[48,3584]{1,0:T(8,128)(2,1)S(1)}, bf16[48,3584]{1,0:T(8,128)(2,1)}, u32[]{:S(2)}, u32[]{:S(2)}) %collective-permute-start) | collective-permute-done | bytes 344096 | tf_op jit(solution)/shard_map/ppermute | solution.py:163
  45.8 4.3 %collective-permute-start.1 = (bf16[48,3584]{1,0:T(8,128)(2,1)}, bf16[48,3584]{1,0:T(8,128)(2,1)}, u32[]{:S(2)}, u32[]{:S(2)}) collective-permute-start(bf16[48,3584]{1,0:T(8,128)(2,1)} %collective-permute-done), channel_id=1, source_target_pairs={{0,2},{2,4},{4,6},{6,7},{7,5},{5,3},{3,1},{1,0},{8,10},{10,12},{12... | collective-permute-start | bytes 1032200 | tf_op jit(solution)/shard_map/ppermute | solution.py:163
  57.7 5.0 %collective-permute-start.2 = (bf16[48,3584]{1,0:T(8,128)(2,1)}, bf16[48,3584]{1,0:T(8,128)(2,1)}, u32[]{:S(2)}, u32[]{:S(2)}) collective-permute-start(bf16[48,3584]{1,0:T(8,128)(2,1)} %collective-permute-done.1), channel_id=1, source_target_pairs={{0,2},{2,4},{4,6},{6,7},{7,5},{5,3},{3,1},{1,0},{8,10},{10,12},{12... | collective-permute-start | bytes 1032200 | tf_op jit(solution)/shard_map/ppermute | solution.py:163
  64.3 5.0 %collective-permute-done.7 = bf16[48,3584]{1,0:T(8,128)(2,1)} collective-permute-done((bf16[48,3584]{1,0:T(8,128)(2,1)}, bf16[48,3584]{1,0:T(8,128)(2,1)}, u32[]{:S(2)}, u32[]{:S(2)}) %collective-permute-start.7) | collective-permute-done | bytes 344096 | tf_op jit(solution)/shard_map/ppermute | solution.py:166
  78.2 5.8 %collective-permute-done.8 = bf16[48,3584]{1,0:T(8,128)(2,1)} collective-permute-done((bf16[48,3584]{1,0:T(8,128)(2,1)}, bf16[48,3584]{1,0:T(8,128)(2,1)}, u32[]{:S(2)}, u32[]{:S(2)}) %collective-permute-start.8) | collective-permute-done | bytes 344096 | tf_op jit(solution)/shard_map/ppermute | solution.py:166
  86.6 3.0 collective-permute-start.9
  89.6 4.4 %collective-permute-start.4 = (bf16[48,3584]{1,0:T(8,128)(2,1)}, bf16[48,3584]{1,0:T(8,128)(2,1)}, u32[]{:S(2)}, u32[]{:S(2)}) collective-permute-start(bf16[48,3584]{1,0:T(8,128)(2,1)} %collective-permute-done.3), channel_id=1, source_target_pairs={{0,2},{2,4},{4,6},{6,7},{7,5},{5,3},{3,1},{1,0},{8,10},{10,12},{12... | collective-permute-start | bytes 1032200 | tf_op jit(solution)/shard_map/ppermute | solution.py:163
  95.7 3.2 collective-permute-done.9
  101.3 3.0 collective-permute-start.10
  104.3 4.1 %collective-permute-start.5 = (bf16[48,3584]{1,0:T(8,128)(2,1)}, bf16[48,3584]{1,0:T(8,128)(2,1)}, u32[]{:S(2)}, u32[]{:S(2)}) collective-permute-start(bf16[48,3584]{1,0:T(8,128)(2,1)} %collective-permute-done.4), channel_id=1, source_target_pairs={{0,2},{2,4},{4,6},{6,7},{7,5},{5,3},{3,1},{1,0},{8,10},{10,12},{12... | collective-permute-start | bytes 1032200 | tf_op jit(solution)/shard_map/ppermute | solution.py:163
  110.1 3.5 collective-permute-done.10
  116.0 3.0 collective-permute-start.11
  120.7 4.0 %collective-permute-start.6 = (bf16[48,3584]{1,0:T(8,128)(2,1)}, bf16[48,3584]{1,0:T(8,128)(2,1)}, u32[]{:S(2)}, u32[]{:S(2)}) collective-permute-start(bf16[48,3584]{1,0:T(8,128)(2,1)} %collective-permute-done.5), channel_id=1, source_target_pairs={{0,2},{2,4},{4,6},{6,7},{7,5},{5,3},{3,1},{1,0},{8,10},{10,12},{12... | collective-permute-start | bytes 1032200 | tf_op jit(solution)/shard_map/ppermute | solution.py:163
  124.8 3.5 collective-permute-done.11
  130.8 3.0 collective-permute-start.12
  135.9 6.5 %collective-permute-done.12 = bf16[48,3584]{1,0:T(8,128)(2,1)} collective-permute-done((bf16[48,3584]{1,0:T(8,128)(2,1)}, bf16[48,3584]{1,0:T(8,128)(2,1)}, u32[]{:S(2)}, u32[]{:S(2)}) %collective-permute-start.12) | collective-permute-done | bytes 344096 | tf_op jit(solution)/shard_map/ppermute | solution.py:166
  147.4 9.0 %collective-permute-done.13 = bf16[48,3584]{1,0:T(8,128)(2,1)} collective-permute-done((bf16[48,3584]{1,0:T(8,128)(2,1)}, bf16[48,3584]{1,0:T(8,128)(2,1)}, u32[]{:S(2)}, u32[]{:S(2)}) %collective-permute-start.13) | collective-permute-done | bytes 344096 | tf_op jit(solution)/shard_map/ppermute | solution.py:166
  159.0 4.6 %all-to-all-start.1 = ((bf16[8,3,2,3584]{3,2,1,0:T(2,128)(2,1)}), bf16[8,3,2,3584]{3,2,1,0:T(2,128)(2,1)S(1)}, u32[]{:S(2)}, u32[]{:S(2)}) async-start(bf16[8,3,2,3584]{3,2,1,0:T(2,128)(2,1)} %reshape.50), calls=%async_computation.1 | async-start | bytes 688128 | tf_op jit(solution)/shard_map/all_to_all | solution.py:137
  163.6 14.3 %all-to-all-done.1 = bf16[8,3,2,3584]{3,2,1,0:T(2,128)(2,1)S(1)} async-done(((bf16[8,3,2,3584]{3,2,1,0:T(2,128)(2,1)}), bf16[8,3,2,3584]{3,2,1,0:T(2,128)(2,1)S(1)}, u32[]{:S(2)}, u32[]{:S(2)}) %all-to-all-start.1) | async-done | bytes 344096 | tf_op jit(solution)/shard_map/all_to_all | solution.py:137
  186.3 18.6 %all_to_all.20 = bf16[8,3,2,3584]{3,2,1,0:T(2,128)(2,1)} all-to-all(bf16[8,3,2,3584]{3,2,1,0:T(2,128)(2,1)S(1)} %reshape.52), channel_id=1, replica_groups={{0,15,16,31,32,47,48,63},{1,14,17,30,33,46,49,62},{2,13,18,29,34,45,50,..., dimensions={0} | all-to-all | bytes 688128 | tf_op jit(solution)/shard_map/all_to_all | solution.py:137
  207.9 11.0 %collective-permute-done.15 = bf16[48,3584]{1,0:T(8,128)(2,1)} collective-permute-done((bf16[48,3584]{1,0:T(8,128)(2,1)S(1)}, bf16[48,3584]{1,0:T(8,128)(2,1)}, u32[]{:S(2)}, u32[]{:S(2)}) %collective-permute-start.15) | collective-permute-done | bytes 344096 | tf_op jit(solution)/shard_map/ppermute | solution.py:163
  224.6 2.8 collective-permute-start.22
  227.5 5.1 %collective-permute-done.16 = bf16[48,3584]{1,0:T(8,128)(2,1)} collective-permute-done((bf16[48,3584]{1,0:T(8,128)(2,1)}, bf16[48,3584]{1,0:T(8,128)(2,1)}, u32[]{:S(2)}, u32[]{:S(2)}) %collective-permute-start.16) | collective-permute-done | bytes 344096 | tf_op jit(solution)/shard_map/ppermute | solution.py:163
  236.5 3.4 collective-permute-done.22
  240.0 2.7 conditional.57
  240.0 2.7 fusion.183
  250.1 7.7 %collective-permute-done.23 = bf16[48,3584]{1,0:T(8,128)(2,1)} collective-permute-done((bf16[48,3584]{1,0:T(8,128)(2,1)}, bf16[48,3584]{1,0:T(8,128)(2,1)}, u32[]{:S(2)}, u32[]{:S(2)}) %collective-permute-start.23) | collective-permute-done | bytes 344096 | tf_op jit(solution)/shard_map/ppermute | solution.py:166
  257.8 2.7 conditional.58
  257.8 2.7 fusion.186
  267.5 6.6 %collective-permute-done.24 = bf16[48,3584]{1,0:T(8,128)(2,1)} collective-permute-done((bf16[48,3584]{1,0:T(8,128)(2,1)}, bf16[48,3584]{1,0:T(8,128)(2,1)}, u32[]{:S(2)}, u32[]{:S(2)}) %collective-permute-start.24) | collective-permute-done | bytes 344096 | tf_op jit(solution)/shard_map/ppermute | solution.py:166
  274.0 2.7 conditional.59
  274.0 2.7 fusion.189
  284.9 3.9 %collective-permute-done.25 = bf16[48,3584]{1,0:T(8,128)(2,1)} collective-permute-done((bf16[48,3584]{1,0:T(8,128)(2,1)}, bf16[48,3584]{1,0:T(8,128)(2,1)}, u32[]{:S(2)}, u32[]{:S(2)}) %collective-permute-start.25) | collective-permute-done | bytes 344096 | tf_op jit(solution)/shard_map/ppermute | solution.py:166
  288.8 2.7 conditional.60
  288.8 2.7 fusion.192
  293.4 4.8 %collective-permute-done.20 = bf16[48,3584]{1,0:T(8,128)(2,1)} collective-permute-done((bf16[48,3584]{1,0:T(8,128)(2,1)}, bf16[48,3584]{1,0:T(8,128)(2,1)}, u32[]{:S(2)}, u32[]{:S(2)}) %collective-permute-start.20) | collective-permute-done | bytes 344096 | tf_op jit(solution)/shard_map/ppermute | solution.py:163
  302.2 3.1 collective-permute-done.26
  305.4 2.7 conditional.61
  305.4 2.7 fusion.195
  310.0 4.6 %collective-permute-done.21 = bf16[48,3584]{1,0:T(8,128)(2,1)} collective-permute-done((bf16[48,3584]{1,0:T(8,128)(2,1)}, bf16[48,3584]{1,0:T(8,128)(2,1)}, u32[]{:S(2)}, u32[]{:S(2)}) %collective-permute-start.21) | collective-permute-done | bytes 344096 | tf_op jit(solution)/shard_map/ppermute | solution.py:163
  316.7 2.9 collective-permute-done.27
  319.6 2.7 conditional.62
  319.6 2.7 fusion.198
  326.2 7.7 %collective-permute-done.28 = bf16[48,3584]{1,0:T(8,128)(2,1)} collective-permute-done((bf16[48,3584]{1,0:T(8,128)(2,1)}, bf16[48,3584]{1,0:T(8,128)(2,1)}, u32[]{:S(2)}, u32[]{:S(2)}) %collective-permute-start.28) | collective-permute-done | bytes 344096 | tf_op jit(solution)/shard_map/ppermute | solution.py:166
  336.0 18.6 %all_to_all.21 = bf16[8,3,2,3584]{3,2,1,0:T(2,128)(2,1)S(1)} all-to-all(bf16[8,3,2,3584]{3,2,1,0:T(2,128)(2,1)S(1)} %reshape.54), channel_id=1, replica_groups={{0,15,16,31,32,47,48,63},{1,14,17,30,33,46,49,62},{2,13,18,29,34,45,50,..., dimensions={0} | all-to-all | bytes 688128 | tf_op jit(solution)/shard_map/all_to_all | solution.py:137
  (136 shorter events, 163.1 us)
Async XLA Ops:
  0.0 38.5 %copy-start = (bf16[1,1,384,384]{3,2,1,0:T(8,128)(2,1)S(1)}, bf16[1,1,384,384]{3,2,1,0:T(8,128)(2,1)}, u32[]{:S(2)}) copy-start(bf16[1,1,384,384]{3,2,1,0:T(8,128)(2,1)} %param.72) | copy-start | bytes 884740
  0.0 50.1 %copy-start.1 = (bf16[1,1,3584,384]{3,2,1,0:T(8,128)(2,1)S(1)}, bf16[1,1,3584,384]{3,2,1,0:T(8,128)(2,1)}, u32[]{:S(2)}) copy-start(bf16[1,1,3584,384]{3,2,1,0:T(8,128)(2,1)} %param.75) | copy-start | bytes 8257540
  3.7 28.4 %all-to-all-start = ((bf16[8,3,2,3584]{3,2,1,0:T(2,128)(2,1)}), bf16[8,3,2,3584]{3,2,1,0:T(2,128)(2,1)}, u32[]{:S(2)}, u32[]{:S(2)}) async-start(bf16[8,3,2,3584]{3,2,1,0:T(2,128)(2,1)} %reshape.48), calls=%async_computation | async-start | bytes 688128 | tf_op jit(solution)/shard_map/all_to_all | solution.py:137
  33.3 12.5 %collective-permute-start = (bf16[48,3584]{1,0:T(8,128)(2,1)S(1)}, bf16[48,3584]{1,0:T(8,128)(2,1)}, u32[]{:S(2)}, u32[]{:S(2)}) collective-permute-start(bf16[48,3584]{1,0:T(8,128)(2,1)S(1)} %reshape.49), channel_id=1, source_target_pairs={{0,2},{2,4},{4,6},{6,7},{7,5},{5,3},{3,1},{1,0},{8,10},{10,12},{12... | collective-permute-start | bytes 1032200 | tf_op jit(solution)/shard_map/ppermute | solution.py:163
  45.8 11.9 %collective-permute-start.1 = (bf16[48,3584]{1,0:T(8,128)(2,1)}, bf16[48,3584]{1,0:T(8,128)(2,1)}, u32[]{:S(2)}, u32[]{:S(2)}) collective-permute-start(bf16[48,3584]{1,0:T(8,128)(2,1)} %collective-permute-done), channel_id=1, source_target_pairs={{0,2},{2,4},{4,6},{6,7},{7,5},{5,3},{3,1},{1,0},{8,10},{10,12},{12... | collective-permute-start | bytes 1032200 | tf_op jit(solution)/shard_map/ppermute | solution.py:163
  54.2 15.1 %collective-permute-start.7 = (bf16[48,3584]{1,0:T(8,128)(2,1)}, bf16[48,3584]{1,0:T(8,128)(2,1)}, u32[]{:S(2)}, u32[]{:S(2)}) collective-permute-start(bf16[48,3584]{1,0:T(8,128)(2,1)} %get-tuple-element.673), channel_id=1, source_target_pairs={{0,2},{2,4},{4,6},{6,7},{7,5},{5,3},{3,1},{1,0},{8,10},{10,12},{12... | collective-permute-start | bytes 1032200 | tf_op jit(solution)/shard_map/ppermute | solution.py:166
  57.7 17.0 %collective-permute-start.2 = (bf16[48,3584]{1,0:T(8,128)(2,1)}, bf16[48,3584]{1,0:T(8,128)(2,1)}, u32[]{:S(2)}, u32[]{:S(2)}) collective-permute-start(bf16[48,3584]{1,0:T(8,128)(2,1)} %collective-permute-done.1), channel_id=1, source_target_pairs={{0,2},{2,4},{4,6},{6,7},{7,5},{5,3},{3,1},{1,0},{8,10},{10,12},{12... | collective-permute-start | bytes 1032200 | tf_op jit(solution)/shard_map/ppermute | solution.py:163
  71.8 12.3 %collective-permute-start.8 = (bf16[48,3584]{1,0:T(8,128)(2,1)}, bf16[48,3584]{1,0:T(8,128)(2,1)}, u32[]{:S(2)}, u32[]{:S(2)}) collective-permute-start(bf16[48,3584]{1,0:T(8,128)(2,1)} %get-tuple-element.674), channel_id=1, source_target_pairs={{0,2},{2,4},{4,6},{6,7},{7,5},{5,3},{3,1},{1,0},{8,10},{10,12},{12... | collective-permute-start | bytes 1032200 | tf_op jit(solution)/shard_map/ppermute | solution.py:166
  74.7 14.9 %collective-permute-start.3 = (bf16[48,3584]{1,0:T(8,128)(2,1)}, bf16[48,3584]{1,0:T(8,128)(2,1)}, u32[]{:S(2)}, u32[]{:S(2)}) collective-permute-start(bf16[48,3584]{1,0:T(8,128)(2,1)} %collective-permute-done.2), channel_id=1, source_target_pairs={{0,2},{2,4},{4,6},{6,7},{7,5},{5,3},{3,1},{1,0},{8,10},{10,12},{12... | collective-permute-start | bytes 1032200 | tf_op jit(solution)/shard_map/ppermute | solution.py:163
  86.6 12.3 %collective-permute-start.9 = (bf16[48,3584]{1,0:T(8,128)(2,1)}, bf16[48,3584]{1,0:T(8,128)(2,1)}, u32[]{:S(2)}, u32[]{:S(2)}) collective-permute-start(bf16[48,3584]{1,0:T(8,128)(2,1)} %get-tuple-element.675), channel_id=1, source_target_pairs={{0,2},{2,4},{4,6},{6,7},{7,5},{5,3},{3,1},{1,0},{8,10},{10,12},{12... | collective-permute-start | bytes 1032200 | tf_op jit(solution)/shard_map/ppermute | solution.py:166
  89.6 14.7 %collective-permute-start.4 = (bf16[48,3584]{1,0:T(8,128)(2,1)}, bf16[48,3584]{1,0:T(8,128)(2,1)}, u32[]{:S(2)}, u32[]{:S(2)}) collective-permute-start(bf16[48,3584]{1,0:T(8,128)(2,1)} %collective-permute-done.3), channel_id=1, source_target_pairs={{0,2},{2,4},{4,6},{6,7},{7,5},{5,3},{3,1},{1,0},{8,10},{10,12},{12... | collective-permute-start | bytes 1032200 | tf_op jit(solution)/shard_map/ppermute | solution.py:163
  101.3 12.3 %collective-permute-start.10 = (bf16[48,3584]{1,0:T(8,128)(2,1)}, bf16[48,3584]{1,0:T(8,128)(2,1)}, u32[]{:S(2)}, u32[]{:S(2)}) collective-permute-start(bf16[48,3584]{1,0:T(8,128)(2,1)} %get-tuple-element.676), channel_id=1, source_target_pairs={{0,2},{2,4},{4,6},{6,7},{7,5},{5,3},{3,1},{1,0},{8,10},{10,12},{12... | collective-permute-start | bytes 1032200 | tf_op jit(solution)/shard_map/ppermute | solution.py:166
  104.3 14.7 %collective-permute-start.5 = (bf16[48,3584]{1,0:T(8,128)(2,1)}, bf16[48,3584]{1,0:T(8,128)(2,1)}, u32[]{:S(2)}, u32[]{:S(2)}) collective-permute-start(bf16[48,3584]{1,0:T(8,128)(2,1)} %collective-permute-done.4), channel_id=1, source_target_pairs={{0,2},{2,4},{4,6},{6,7},{7,5},{5,3},{3,1},{1,0},{8,10},{10,12},{12... | collective-permute-start | bytes 1032200 | tf_op jit(solution)/shard_map/ppermute | solution.py:163
  116.0 12.3 %collective-permute-start.11 = (bf16[48,3584]{1,0:T(8,128)(2,1)}, bf16[48,3584]{1,0:T(8,128)(2,1)}, u32[]{:S(2)}, u32[]{:S(2)}) collective-permute-start(bf16[48,3584]{1,0:T(8,128)(2,1)} %get-tuple-element.677), channel_id=1, source_target_pairs={{0,2},{2,4},{4,6},{6,7},{7,5},{5,3},{3,1},{1,0},{8,10},{10,12},{12... | collective-permute-start | bytes 1032200 | tf_op jit(solution)/shard_map/ppermute | solution.py:166
  120.7 13.5 %collective-permute-start.6 = (bf16[48,3584]{1,0:T(8,128)(2,1)}, bf16[48,3584]{1,0:T(8,128)(2,1)}, u32[]{:S(2)}, u32[]{:S(2)}) collective-permute-start(bf16[48,3584]{1,0:T(8,128)(2,1)} %collective-permute-done.5), channel_id=1, source_target_pairs={{0,2},{2,4},{4,6},{6,7},{7,5},{5,3},{3,1},{1,0},{8,10},{10,12},{12... | collective-permute-start | bytes 1032200 | tf_op jit(solution)/shard_map/ppermute | solution.py:163
  130.8 11.6 %collective-permute-start.12 = (bf16[48,3584]{1,0:T(8,128)(2,1)}, bf16[48,3584]{1,0:T(8,128)(2,1)}, u32[]{:S(2)}, u32[]{:S(2)}) collective-permute-start(bf16[48,3584]{1,0:T(8,128)(2,1)} %get-tuple-element.678), channel_id=1, source_target_pairs={{0,2},{2,4},{4,6},{6,7},{7,5},{5,3},{3,1},{1,0},{8,10},{10,12},{12... | collective-permute-start | bytes 1032200 | tf_op jit(solution)/shard_map/ppermute | solution.py:166
  144.8 11.6 %collective-permute-start.13 = (bf16[48,3584]{1,0:T(8,128)(2,1)}, bf16[48,3584]{1,0:T(8,128)(2,1)}, u32[]{:S(2)}, u32[]{:S(2)}) collective-permute-start(bf16[48,3584]{1,0:T(8,128)(2,1)} %get-tuple-element.679), channel_id=1, source_target_pairs={{0,2},{2,4},{4,6},{6,7},{7,5},{5,3},{3,1},{1,0},{8,10},{10,12},{12... | collective-permute-start | bytes 1032200 | tf_op jit(solution)/shard_map/ppermute | solution.py:166
  156.4 7.2 %copy-start.5 = (f32[2,1,32,1]{2,3,1,0:T(1,128)S(1)}, f32[2,1,32,1]{2,3,1,0:T(1,128)}, u32[]{:S(2)}) copy-start(f32[2,1,32,1]{2,3,1,0:T(1,128)} %param.74) | copy-start | bytes 772
  159.0 18.9 %all-to-all-start.1 = ((bf16[8,3,2,3584]{3,2,1,0:T(2,128)(2,1)}), bf16[8,3,2,3584]{3,2,1,0:T(2,128)(2,1)S(1)}, u32[]{:S(2)}, u32[]{:S(2)}) async-start(bf16[8,3,2,3584]{3,2,1,0:T(2,128)(2,1)} %reshape.50), calls=%async_computation.1 | async-start | bytes 688128 | tf_op jit(solution)/shard_map/all_to_all | solution.py:137
  180.1 3.4 copy-start.2
  180.1 3.4 collective-permute-start.14
  183.5 0.7 copy-start.4
  206.0 12.9 %collective-permute-start.15 = (bf16[48,3584]{1,0:T(8,128)(2,1)S(1)}, bf16[48,3584]{1,0:T(8,128)(2,1)}, u32[]{:S(2)}, u32[]{:S(2)}) collective-permute-start(bf16[48,3584]{1,0:T(8,128)(2,1)S(1)} %reshape.53), channel_id=1, source_target_pairs={{0,2},{2,4},{4,6},{6,7},{7,5},{5,3},{3,1},{1,0},{8,10},{10,12},{12... | collective-permute-start | bytes 1032200 | tf_op jit(solution)/shard_map/ppermute | solution.py:163
  219.0 13.6 %collective-permute-start.16 = (bf16[48,3584]{1,0:T(8,128)(2,1)}, bf16[48,3584]{1,0:T(8,128)(2,1)}, u32[]{:S(2)}, u32[]{:S(2)}) collective-permute-start(bf16[48,3584]{1,0:T(8,128)(2,1)} %collective-permute-done.15), channel_id=1, source_target_pairs={{0,2},{2,4},{4,6},{6,7},{7,5},{5,3},{3,1},{1,0},{8,10},{10,12},{12... | collective-permute-start | bytes 1032200 | tf_op jit(solution)/shard_map/ppermute | solution.py:163
  224.6 15.4 %collective-permute-start.22 = (bf16[48,3584]{1,0:T(8,128)(2,1)}, bf16[48,3584]{1,0:T(8,128)(2,1)}, u32[]{:S(2)}, u32[]{:S(2)}) collective-permute-start(bf16[48,3584]{1,0:T(8,128)(2,1)} %get-tuple-element.689), channel_id=1, source_target_pairs={{0,2},{2,4},{4,6},{6,7},{7,5},{5,3},{3,1},{1,0},{8,10},{10,12},{12... | collective-permute-start | bytes 1032200 | tf_op jit(solution)/shard_map/ppermute | solution.py:166
  234.6 11.6 %collective-permute-start.17 = (bf16[48,3584]{1,0:T(8,128)(2,1)}, bf16[48,3584]{1,0:T(8,128)(2,1)}, u32[]{:S(2)}, u32[]{:S(2)}) collective-permute-start(bf16[48,3584]{1,0:T(8,128)(2,1)} %collective-permute-done.16), channel_id=1, source_target_pairs={{0,2},{2,4},{4,6},{6,7},{7,5},{5,3},{3,1},{1,0},{8,10},{10,12},{12... | collective-permute-start | bytes 1032200 | tf_op jit(solution)/shard_map/ppermute | solution.py:163
  242.7 15.1 %collective-permute-start.23 = (bf16[48,3584]{1,0:T(8,128)(2,1)}, bf16[48,3584]{1,0:T(8,128)(2,1)}, u32[]{:S(2)}, u32[]{:S(2)}) collective-permute-start(bf16[48,3584]{1,0:T(8,128)(2,1)} %get-tuple-element.690), channel_id=1, source_target_pairs={{0,2},{2,4},{4,6},{6,7},{7,5},{5,3},{3,1},{1,0},{8,10},{10,12},{12... | collective-permute-start | bytes 1032200 | tf_op jit(solution)/shard_map/ppermute | solution.py:166
  248.2 15.3 %collective-permute-start.18 = (bf16[48,3584]{1,0:T(8,128)(2,1)}, bf16[48,3584]{1,0:T(8,128)(2,1)}, u32[]{:S(2)}, u32[]{:S(2)}) collective-permute-start(bf16[48,3584]{1,0:T(8,128)(2,1)} %collective-permute-done.17), channel_id=1, source_target_pairs={{0,2},{2,4},{4,6},{6,7},{7,5},{5,3},{3,1},{1,0},{8,10},{10,12},{12... | collective-permute-start | bytes 1032200 | tf_op jit(solution)/shard_map/ppermute | solution.py:163
  260.4 13.6 %collective-permute-start.24 = (bf16[48,3584]{1,0:T(8,128)(2,1)}, bf16[48,3584]{1,0:T(8,128)(2,1)}, u32[]{:S(2)}, u32[]{:S(2)}) collective-permute-start(bf16[48,3584]{1,0:T(8,128)(2,1)} %get-tuple-element.691), channel_id=1, source_target_pairs={{0,2},{2,4},{4,6},{6,7},{7,5},{5,3},{3,1},{1,0},{8,10},{10,12},{12... | collective-permute-start | bytes 1032200 | tf_op jit(solution)/shard_map/ppermute | solution.py:166
  265.5 15.4 %collective-permute-start.19 = (bf16[48,3584]{1,0:T(8,128)(2,1)}, bf16[48,3584]{1,0:T(8,128)(2,1)}, u32[]{:S(2)}, u32[]{:S(2)}) collective-permute-start(bf16[48,3584]{1,0:T(8,128)(2,1)} %collective-permute-done.18), channel_id=1, source_target_pairs={{0,2},{2,4},{4,6},{6,7},{7,5},{5,3},{3,1},{1,0},{8,10},{10,12},{12... | collective-permute-start | bytes 1032200 | tf_op jit(solution)/shard_map/ppermute | solution.py:163
  276.7 12.1 %collective-permute-start.25 = (bf16[48,3584]{1,0:T(8,128)(2,1)}, bf16[48,3584]{1,0:T(8,128)(2,1)}, u32[]{:S(2)}, u32[]{:S(2)}) collective-permute-start(bf16[48,3584]{1,0:T(8,128)(2,1)} %get-tuple-element.692), channel_id=1, source_target_pairs={{0,2},{2,4},{4,6},{6,7},{7,5},{5,3},{3,1},{1,0},{8,10},{10,12},{12... | collective-permute-start | bytes 1032200 | tf_op jit(solution)/shard_map/ppermute | solution.py:166
  283.0 15.2 %collective-permute-start.20 = (bf16[48,3584]{1,0:T(8,128)(2,1)}, bf16[48,3584]{1,0:T(8,128)(2,1)}, u32[]{:S(2)}, u32[]{:S(2)}) collective-permute-start(bf16[48,3584]{1,0:T(8,128)(2,1)} %collective-permute-done.19), channel_id=1, source_target_pairs={{0,2},{2,4},{4,6},{6,7},{7,5},{5,3},{3,1},{1,0},{8,10},{10,12},{12... | collective-permute-start | bytes 1032200 | tf_op jit(solution)/shard_map/ppermute | solution.py:163
  291.5 13.9 %collective-permute-start.26 = (bf16[48,3584]{1,0:T(8,128)(2,1)}, bf16[48,3584]{1,0:T(8,128)(2,1)}, u32[]{:S(2)}, u32[]{:S(2)}) collective-permute-start(bf16[48,3584]{1,0:T(8,128)(2,1)} %get-tuple-element.693), channel_id=1, source_target_pairs={{0,2},{2,4},{4,6},{6,7},{7,5},{5,3},{3,1},{1,0},{8,10},{10,12},{12... | collective-permute-start | bytes 1032200 | tf_op jit(solution)/shard_map/ppermute | solution.py:166
  300.3 14.3 %collective-permute-start.21 = (bf16[48,3584]{1,0:T(8,128)(2,1)}, bf16[48,3584]{1,0:T(8,128)(2,1)}, u32[]{:S(2)}, u32[]{:S(2)}) collective-permute-start(bf16[48,3584]{1,0:T(8,128)(2,1)} %collective-permute-done.20), channel_id=1, source_target_pairs={{0,2},{2,4},{4,6},{6,7},{7,5},{5,3},{3,1},{1,0},{8,10},{10,12},{12... | collective-permute-start | bytes 1032200 | tf_op jit(solution)/shard_map/ppermute | solution.py:163
  308.0 11.6 %collective-permute-start.27 = (bf16[48,3584]{1,0:T(8,128)(2,1)}, bf16[48,3584]{1,0:T(8,128)(2,1)}, u32[]{:S(2)}, u32[]{:S(2)}) collective-permute-start(bf16[48,3584]{1,0:T(8,128)(2,1)} %get-tuple-element.694), channel_id=1, source_target_pairs={{0,2},{2,4},{4,6},{6,7},{7,5},{5,3},{3,1},{1,0},{8,10},{10,12},{12... | collective-permute-start | bytes 1032200 | tf_op jit(solution)/shard_map/ppermute | solution.py:166
  322.3 11.6 %collective-permute-start.28 = (bf16[48,3584]{1,0:T(8,128)(2,1)}, bf16[48,3584]{1,0:T(8,128)(2,1)}, u32[]{:S(2)}, u32[]{:S(2)}) collective-permute-start(bf16[48,3584]{1,0:T(8,128)(2,1)} %get-tuple-element.695), channel_id=1, source_target_pairs={{0,2},{2,4},{4,6},{6,7},{7,5},{5,3},{3,1},{1,0},{8,10},{10,12},{12... | collective-permute-start | bytes 1032200 | tf_op jit(solution)/shard_map/ppermute | solution.py:166
  335.8 20.1 %copy-start.3 = (bf16[32,3584]{1,0:T(8,128)(2,1)S(1)}, bf16[32,3584]{1,0:T(8,128)(2,1)}, u32[]{:S(2)}) copy-start(bf16[32,3584]{1,0:T(8,128)(2,1)} %copy-done.2) | copy-start | bytes 688132
